TPU v7x, 512 devices: a whole 4x8x8 slice. The times are simulated.
512 devices in a mesh: gx: 32 (over z, x), gy: 16 (over y, core).
Axes of the slice: x: 4, y: 8, z: 8, core: 2. Of those that a mesh axis runs over, the one named last changes fastest.
Arguments:
- vel0: bfloat16 [2, 8192, 4096], P(None, 'gx', 'gy'), may hold values from -6 to 6
- visc: float32 [8192, 4096], P('gx', 'gy'), may hold values from 0.1 to 1
- fric: float32 [8192, 4096], P('gx', 'gy'), may hold values from 0.5 to 5
- drive: bfloat16 [2, 8192, 4096], P(None, 'gx', 'gy'), may hold values from -6 to 6
- scene_obs: bfloat16 [16, 512, 2, 128, 128], P('gy', 'gx'), may hold values from -6 to 6
- scene_weight: bfloat16 [16, 512], P('gy', 'gx'), may hold values from 0.5 to 4
- scene_owner: int32 [16, 512, 1], P('gy', 'gx'), may hold values from 0 to 31; in each aligned block of 16 rows (0 to 15, 16 to 31, ..., all dimensions but the last counted through in order) at most 2 rows name the same one
- scene_slot: int32 [16, 512], P('gy', 'gx'), may hold values from 0 to 3
- ice_mask: int32 [64, 32], P('gx', 'gy'), may hold values 0 or 1
Outputs:
- grad_fric: float32 [8192, 4096], P('gx', 'gy')
Inputs may be any that keep to these rules, and one draw needn't show every extreme that they name: `scene_owner`: among one device's 16 scenes at most 2 name the same owner, and in some device one owner is named exactly 2 times.
All inputs are finite; a program needn't handle non-finite values. No bound on the sum of `ice_mask` on one device may be relied on, other than what follows from the above.
Results may differ from a plain program's by a relative error of at most 0.0003.
Values may be sent and summed in bfloat16 or wider, within the bound.
A program may use at most 64 MiB of HBM per device.

v0:
```python
import jax
import jax.numpy as jnp
from jax import lax
from jax.sharding import PartitionSpec as P

CAP = 2


OMEGA = 0.6


def from_behind(value, axis, steps):
    count = lax.axis_size(axis)
    first, last = (max(0, -steps), min(count, count - steps))
    return lax.ppermute(value, axis, [(source, source + steps) for source in range(first, last)])


def stress_image(field, visc):
    above_x = from_behind(field[:, :1, :], "gx", -1)
    above_y = from_behind(field[:, :, :1], "gy", -1)
    along_x = jnp.concatenate([field[:, 1:, :], above_x], axis=1) - field
    along_y = jnp.concatenate([field[:, :, 1:], above_y], axis=2) - field
    sxx = visc * (4.0 * along_x[0] + 2.0 * along_y[1])
    syy = visc * (4.0 * along_y[1] + 2.0 * along_x[0])
    sxy = visc * (along_y[0] + along_x[1])
    below_x = from_behind(jnp.stack([sxx[-1], sxy[-1]]), "gx", 1)
    below_y = from_behind(jnp.stack([sxy[:, -1], syy[:, -1]]), "gy", 1)
    push_u = (
        jnp.concatenate([below_x[0:1], sxx[:-1]], axis=0)
        - sxx
        + jnp.concatenate([below_y[0][:, None], sxy[:, :-1]], axis=1)
        - sxy
    )
    push_v = (
        jnp.concatenate([below_x[1:2], sxy[:-1]], axis=0)
        - sxy
        + jnp.concatenate([below_y[1][:, None], syy[:, :-1]], axis=1)
        - syy
    )
    return jnp.stack([push_u, push_v])


def spread_tiles(values, tiles_x, tiles_y, tile):
    wide = jnp.broadcast_to(values.reshape(tiles_x, 1, tiles_y, 1), (tiles_x, tile, tiles_y, tile))
    return wide.reshape(tiles_x * tile, tiles_y * tile)


def body(vel0, visc, fric, drive, scene_obs, scene_weight, scene_owner, scene_slot, ice_mask):
    cells_x, cells_y = visc.shape
    tile = scene_obs.shape[-1]
    tiles_x = cells_x // tile
    tiles_y = cells_y // tile
    slot_count = tiles_x * tiles_y
    visc_row = from_behind(visc[-1:, :], "gx", 1)
    visc_col = from_behind(visc[:, -1:], "gy", 1)
    visc_x = jnp.concatenate([visc_row, visc[:-1]], axis=0)
    visc_y = jnp.concatenate([visc_col, visc[:, :-1]], axis=1)
    diag = jnp.stack([5.0 * visc + 4.0 * visc_x + visc_y, 5.0 * visc + visc_x + 4.0 * visc_y])
    relax = 1.0 / (diag + fric)
    owners = scene_owner[0, :, 0]
    slots = scene_slot[0]
    weights = scene_weight[0]
    observed = scene_obs[0]
    count = owners.shape[0]
    groups = lax.axis_size("gx")
    places = groups * CAP
    order = jnp.arange(count, dtype=jnp.int32)
    same_owner = owners[:, None] == owners[None, :]
    earlier = order[None, :] < order[:, None]
    rank = jnp.sum(jnp.logical_and(same_owner, earlier), axis=1)
    target = owners * CAP + rank
    place_mask = target[None, :] == jnp.arange(places, dtype=jnp.int32)[:, None]
    place_table = place_mask.astype(jnp.bfloat16)
    obs_buffer = jnp.dot(
        place_table, observed.reshape(count, -1), preferred_element_type=jnp.float32
    )
    obs_buffer = obs_buffer.astype(jnp.bfloat16)
    weight_buffer = jnp.dot(place_table, weights[:, None], preferred_element_type=jnp.float32)[
        :, 0
    ].astype(jnp.bfloat16)
    slot_buffer = jnp.sum(jnp.where(place_mask, slots[None, :], 0), axis=1)
    slot_range = jnp.arange(slot_count, dtype=jnp.int32)
    start = vel0.astype(jnp.float32)
    force = drive.astype(jnp.float32)
    first_res = force - stress_image(start, visc) - fric * start
    first = start + OMEGA * relax * first_res
    second_res = force - stress_image(first, visc) - fric * first
    second = first + OMEGA * relax * second_res
    got_obs, got_weight, got_slot = (
        lax.all_to_all(
            obs_buffer.reshape(places, 2, tile, tile), "gx", split_axis=0, concat_axis=0, tiled=True
        ),
        lax.all_to_all(weight_buffer, "gx", split_axis=0, concat_axis=0, tiled=True),
        lax.all_to_all(slot_buffer, "gx", split_axis=0, concat_axis=0, tiled=True),
    )
    picker = jnp.where(
        got_slot[:, None] == slot_range[None, :], got_weight[:, None], jnp.zeros((), jnp.bfloat16)
    )
    summed = jnp.dot(
        picker.T, got_obs.reshape(got_obs.shape[0], -1), preferred_element_type=jnp.float32
    )
    tile_weight = jnp.sum(picker.astype(jnp.float32), axis=0)
    obs_sum = (
        summed.reshape(tiles_x, tiles_y, 2, tile, tile)
        .transpose(2, 0, 3, 1, 4)
        .reshape(2, cells_x, cells_y)
    )
    weight_cell = spread_tiles(tile_weight, tiles_x, tiles_y, tile)
    ice = spread_tiles(ice_mask.astype(jnp.float32), tiles_x, tiles_y, tile)
    misfit_grad = ice * (weight_cell * second - obs_sum)
    lift_two = OMEGA * relax * misfit_grad
    back = misfit_grad - stress_image(lift_two, visc) - fric * lift_two
    lift_one = OMEGA * relax * back
    part_one = jnp.sum(lift_one * (relax * first_res + start), axis=0)
    part_two = jnp.sum(lift_two * (relax * second_res + first), axis=0)
    return -ice * (part_one + part_two)


def solution(mesh):
    placed = (
        P(None, "gx", "gy"),
        P("gx", "gy"),
        P("gx", "gy"),
        P(None, "gx", "gy"),
        P("gy", "gx", None, None, None),
        P("gy", "gx"),
        P("gy", "gx", None),
        P("gy", "gx"),
        P("gx", "gy"),
    )
    return jax.shard_map(body, mesh=mesh, in_specs=placed, out_specs=P("gx", "gy"), check_vma=False)
```

profile of v0, /device:TPU:272, one launch (start us, length us, event | category | flops | bytes accessed | tf_op | source)
XLA Modules:
  0.0 204.9 jit_solution(2712226502158221784)
XLA Ops:
  0.0 0.9 convert_reduce_fusion
  0.9 0.7 multiply_add_fusion.2
  1.6 0.7 bitcast_convert_fusion
  2.2 0.2 fusion.39
  2.5 0.7 copy.31
  3.2 9.9 %all-to-all-start.1 = ((bf16[32,2,1]{1,2,0:T(2,128)(2,1)}), bf16[32,2,1]{1,2,0:T(2,128)(2,1)S(1)}, u32[]{:S(2)}, u32[]{:S(2)}) async-start(bf16[32,2,1]{1,2,0:T(2,128)(2,1)} %copy.31), calls=%async_computation.1 | async-start | bytes 32768 | tf_op jit(solution)/shard_map/all_to_all | solution.py:93
  13.1 0.7 select_reduce_fusion
  13.8 1.5 reshape_squeeze.3
  15.4 0.7 all_to_all.13
  16.1 1.8 all-to-all-done.1
  17.9 8.8 %all-to-all-start = ((s32[32,2,1]{1,2,0:T(1,128)}), s32[32,2,1]{1,2,0:T(1,128)S(1)}, u32[]{:S(2)}, u32[]{:S(2)}) async-start(s32[32,2,1]{1,2,0:T(1,128)} %bitcast.5), calls=%async_computation | async-start | bytes 32768 | tf_op jit(solution)/shard_map/all_to_all | solution.py:94
  26.7 1.4 fusion.3
  28.1 3.1 %copy.48 = bf16[8,8,256,128]{3,2,1,0:T(8,128)(2,1)} copy(bf16[8,8,256,128]{3,1,2,0:T(8,128)(2,1)S(1)} %fusion.3) | data formatting | bytes 8388608
  31.2 0.2 all-to-all-done
  31.4 9.9 %all-to-all-start.2 = ((bf16[64,2,128,128]{3,2,1,0:T(8,128)(2,1)}), bf16[64,2,128,128]{3,2,1,0:T(8,128)(2,1)}, u32[]{:S(2)}, u32[]{:S(2)}) async-start(bf16[64,2,128,128]{3,2,1,0:T(8,128)(2,1)} %bitcast.126), calls=%async_computation.2 | async-start | bytes 8388608 | tf_op jit(solution)/shard_map/all_to_all | solution.py:90
  41.3 3.4 %collective-permute-start = (f32[1,256]{1,0:T(1,128)S(1)}, f32[1,256]{1,0:T(1,128)S(1)}, u32[]{:S(2)}, u32[]{:S(2)}) collective-permute-start(f32[1,256]{1,0:T(1,128)S(1)} %slice.198), channel_id=1, source_target_pairs={{0,16},{16,32},{32,48},{48,64},{64,80},{80,96},{96,112},{112,128},... | collective-permute-start | bytes 3080 | tf_op jit(solution)/shard_map/ppermute | solution.py:15
  44.8 1.9 collective-permute-start.1
  46.8 5.8 %collective-permute-start.2 = (f32[2,1,256]{2,1,0:T(1,128)S(1)}, f32[2,1,256]{2,1,0:T(1,128)S(1)}, u32[]{:S(2)}, u32[]{:S(2)}) collective-permute-start(f32[2,1,256]{2,1,0:T(1,128)S(1)} %slice.263), channel_id=1, source_target_pairs={{16,0},{32,16},{48,32},{64,48},{80,64},{96,80},{112,96},{128,112},... | collective-permute-start | bytes 6152 | tf_op jit(solution)/shard_map/ppermute | solution.py:15
  52.6 3.4 %collective-permute-start.3 = (f32[2,256,1]{2,1,0:T(8,128)S(1)}, f32[2,256,1]{2,1,0:T(8,128)S(1)}, u32[]{:S(2)}, u32[]{:S(2)}) collective-permute-start(f32[2,256,1]{2,1,0:T(8,128)S(1)} %slice.266), channel_id=1, source_target_pairs={{1,0},{2,1},{3,2},{4,3},{5,4},{6,5},{7,6},{8,7},{9,8},{10,9},{11,1... | collective-permute-start | bytes 6152 | tf_op jit(solution)/shard_map/ppermute | solution.py:15
  56.4 0.5 broadcast.131
  56.9 0.7 reduce.18
  57.9 67.1 %collective-permute-done.2 = f32[2,1,256]{2,1,0:T(1,128)S(1)} collective-permute-done((f32[2,1,256]{2,1,0:T(1,128)S(1)}, f32[2,1,256]{2,1,0:T(1,128)S(1)}, u32[]{:S(2)}, u32[]{:S(2)}) %collective-permute-start.2) | collective-permute-done | bytes 2080 | tf_op jit(solution)/shard_map/ppermute | solution.py:15
  125.2 6.9 %collective-permute-done = f32[1,256]{1,0:T(1,128)S(1)} collective-permute-done((f32[1,256]{1,0:T(1,128)S(1)}, f32[1,256]{1,0:T(1,128)S(1)}, u32[]{:S(2)}, u32[]{:S(2)}) %collective-permute-start) | collective-permute-done | bytes 1056 | tf_op jit(solution)/shard_map/ppermute | solution.py:15
  132.1 0.2 add_bitcast_fusion.1
  132.3 0.2 slice_reduce_fusion.4
  132.6 1.9 collective-permute-start.5
  134.5 1.9 collective-permute-start.4
  136.5 1.0 collective-permute-done.5
  137.8 5.5 %collective-permute-done.4 = f32[2,256]{1,0:T(2,128)S(1)} collective-permute-done((f32[2,256]{1,0:T(2,128)S(1)}, f32[2,256]{1,0:T(2,128)S(1)}, u32[]{:S(2)}, u32[]{:S(2)}) %collective-permute-start.4) | collective-permute-done | bytes 2080 | tf_op jit(solution)/shard_map/ppermute | solution.py:15
  143.3 0.2 fusion.23
  143.6 0.2 convert_add_fusion.1
  143.8 1.9 collective-permute-start.6
  145.7 2.5 %collective-permute-start.7 = (f32[2,256,1]{2,1,0:T(8,128)S(1)}, f32[2,256,1]{2,1,0:T(8,128)S(1)}, u32[]{:S(2)}, u32[]{:S(2)}) collective-permute-start(f32[2,256,1]{2,1,0:T(8,128)S(1)} %slice.286), channel_id=1, source_target_pairs={{1,0},{2,1},{3,2},{4,3},{5,4},{6,5},{7,6},{8,7},{9,8},{10,9},{11,1... | collective-permute-start | bytes 6152 | tf_op jit(solution)/shard_map/ppermute | solution.py:15
  148.5 0.7 copy-done.4
  149.3 0.8 copy_bitcast_fusion
  150.1 0.2 slice.285
  150.3 1.8 collective-permute-done.7
  152.1 0.1 maximum_subtract_fusion
  152.4 0.2 slice_reduce_fusion.3
  152.6 0.2 slice_reduce_fusion.2
  152.8 3.8 %collective-permute-start.9 = (f32[2,256]{1,0:T(2,128)S(1)}, f32[2,256]{1,0:T(2,128)S(1)}, u32[]{:S(2)}, u32[]{:S(2)}) collective-permute-start(f32[2,256]{1,0:T(2,128)S(1)} %pad_maximum_fusion.5), channel_id=1, source_target_pairs={{0,1},{1,2},{2,3},{3,4},{4,5},{5,6},{6,7},{7,8},{8,9},{9,10},{10,1... | collective-permute-start | bytes 6152 | tf_op jit(solution)/shard_map/ppermute | solution.py:15
  156.6 3.8 %collective-permute-start.8 = (f32[2,256]{1,0:T(2,128)S(1)}, f32[2,256]{1,0:T(2,128)S(1)}, u32[]{:S(2)}, u32[]{:S(2)}) collective-permute-start(f32[2,256]{1,0:T(2,128)S(1)} %pad_maximum_fusion.4), channel_id=1, source_target_pairs={{0,16},{16,32},{32,48},{48,64},{64,80},{80,96},{96,112},{112,128},... | collective-permute-start | bytes 6152 | tf_op jit(solution)/shard_map/ppermute | solution.py:15
  160.7 4.7 %collective-permute-done.8 = f32[2,256]{1,0:T(2,128)S(1)} collective-permute-done((f32[2,256]{1,0:T(2,128)S(1)}, f32[2,256]{1,0:T(2,128)S(1)}, u32[]{:S(2)}, u32[]{:S(2)}) %collective-permute-start.8) | collective-permute-done | bytes 2080 | tf_op jit(solution)/shard_map/ppermute | solution.py:15
  165.4 0.9 fusion.29
  166.3 5.0 %copy.63 = bf16[8,8,256,128]{3,1,2,0:T(8,128)(2,1)S(1)} copy(bf16[8,8,256,128]{3,2,1,0:T(8,128)(2,1)} %bitcast.52) | data formatting | bytes 8388608
  171.3 1.2 copy.50
  172.4 2.4 %fusion.4 = f32[2,2,128,2,128]{4,3,2,0,1:T(2,128)S(1)} fusion(bf16[2,128,128,64]{2,1,0,3:T(8,128)(2,1)S(1)} %bitcast.127, s32[2,2]{1,0:T(2,128)S(1)} %multiply_add_fusion.1, s32[64]{0:T(128)S(1)} %eq.90, bf16[64]{0:T(256)(128)(2,1)S(1)} %broadcast_in_dim.59), kind=kOutput, calls=%fused_computation.6 | convolution fusion | flops 16777728 | bytes 4718992 | tf_op jit(solution)/shard_map/dot_general | solution.py:99
  174.9 0.4 reshape.126
  175.4 2.1 %multiply_reduce_fusion = (f32[256,256]{1,0:T(8,128)}, f32[2,256,256]{2,1,0:T(8,128)S(1)}) fusion(f32[2,256,256]{2,1,0:T(8,128)S(1)} %convert_add_fusion.1, f32[1,256,256]{2,1,0:T(8,128)} %get-tuple-element.25, f32[1,256,256]{2,1,0:T(8,128)S(1)} %get-tuple-element.24, bf16[2,256,256]{2,1,0:T(8,128)(2,1)S(1)} %copy-done.7, f32[256,256]{1,0:T(8,128)S(1)} %copy-done.6, ...), kind=kLoop, calls=%fused_computation.27 | loop fusion | flops 2424832 | bytes 3932160 | tf_op jit(solution)/shard_map/reduce_sum | solution.py:115
  177.5 1.9 collective-permute-start.10
  179.5 1.9 collective-permute-start.11
  181.4 0.2 slice.305
  181.6 1.4 collective-permute-done.10
  183.0 2.2 %collective-permute-done.11 = f32[2,256,1]{2,1,0:T(8,128)S(1)} collective-permute-done((f32[2,256,1]{2,1,0:T(8,128)S(1)}, f32[2,256,1]{2,1,0:T(8,128)S(1)}, u32[]{:S(2)}, u32[]{:S(2)}) %collective-permute-start.11) | collective-permute-done | bytes 2080 | tf_op jit(solution)/shard_map/ppermute | solution.py:15
  185.3 0.1 maximum_subtract_fusion.2
  185.5 0.2 slice_reduce_fusion.1
  185.7 0.2 slice_reduce_fusion
  185.9 6.2 %collective-permute-start.13 = (f32[2,256]{1,0:T(2,128)S(1)}, f32[2,256]{1,0:T(2,128)S(1)}, u32[]{:S(2)}, u32[]{:S(2)}) collective-permute-start(f32[2,256]{1,0:T(2,128)S(1)} %pad_maximum_fusion.7), channel_id=1, source_target_pairs={{0,1},{1,2},{2,3},{3,4},{4,5},{5,6},{6,7},{7,8},{8,9},{9,10},{10,1... | collective-permute-start | bytes 6152 | tf_op jit(solution)/shard_map/ppermute | solution.py:15
  192.1 3.9 %collective-permute-start.12 = (f32[2,256]{1,0:T(2,128)S(1)}, f32[2,256]{1,0:T(2,128)S(1)}, u32[]{:S(2)}, u32[]{:S(2)}) collective-permute-start(f32[2,256]{1,0:T(2,128)S(1)} %pad_maximum_fusion.6), channel_id=1, source_target_pairs={{0,16},{16,32},{32,48},{48,64},{64,80},{80,96},{96,112},{112,128},... | collective-permute-start | bytes 6152 | tf_op jit(solution)/shard_map/ppermute | solution.py:15
  196.2 0.8 copy.39
  197.0 3.9 %collective-permute-done.12 = f32[2,256]{1,0:T(2,128)S(1)} collective-permute-done((f32[2,256]{1,0:T(2,128)S(1)}, f32[2,256]{1,0:T(2,128)S(1)}, u32[]{:S(2)}, u32[]{:S(2)}) %collective-permute-start.12) | collective-permute-done | bytes 2080 | tf_op jit(solution)/shard_map/ppermute | solution.py:15
  200.9 1.1 fusion.35
  202.0 2.0 fusion.9
  204.1 0.8 add_multiply_fusion
  (77 shorter events, 2.5 us)
Async XLA Ops:
  3.2 14.6 %all-to-all-start.1 = ((bf16[32,2,1]{1,2,0:T(2,128)(2,1)}), bf16[32,2,1]{1,2,0:T(2,128)(2,1)S(1)}, u32[]{:S(2)}, u32[]{:S(2)}) async-start(bf16[32,2,1]{1,2,0:T(2,128)(2,1)} %copy.31), calls=%async_computation.1 | async-start | bytes 32768 | tf_op jit(solution)/shard_map/all_to_all | solution.py:93
  17.9 13.5 %all-to-all-start = ((s32[32,2,1]{1,2,0:T(1,128)}), s32[32,2,1]{1,2,0:T(1,128)S(1)}, u32[]{:S(2)}, u32[]{:S(2)}) async-start(s32[32,2,1]{1,2,0:T(1,128)} %bitcast.5), calls=%async_computation | async-start | bytes 32768 | tf_op jit(solution)/shard_map/all_to_all | solution.py:94
  31.4 9.9 %copy-start.1 = (f32[256,256]{1,0:T(8,128)S(1)}, f32[256,256]{1,0:T(8,128)}, u32[]{:S(2)}) copy-start(f32[256,256]{1,0:T(8,128)} %param.10) | copy-start | bytes 786436
  31.4 15.3 %copy-start = (bf16[2,256,256]{2,1,0:T(8,128)(2,1)S(1)}, bf16[2,256,256]{2,1,0:T(8,128)(2,1)}, u32[]{:S(2)}) copy-start(bf16[2,256,256]{2,1,0:T(8,128)(2,1)} %param.9) | copy-start | bytes 786436
  31.4 24.8 %copy-start.10 = (s32[2,2]{1,0:T(2,128)S(1)}, s32[2,2]{1,0:T(2,128)}, u32[]{:S(2)}) copy-start(s32[2,2]{1,0:T(2,128)} %param.17) | copy-start | bytes 52
  31.4 134.9 %all-to-all-start.2 = ((bf16[64,2,128,128]{3,2,1,0:T(8,128)(2,1)}), bf16[64,2,128,128]{3,2,1,0:T(8,128)(2,1)}, u32[]{:S(2)}, u32[]{:S(2)}) async-start(bf16[64,2,128,128]{3,2,1,0:T(8,128)(2,1)} %bitcast.126), calls=%async_computation.2 | async-start | bytes 8388608 | tf_op jit(solution)/shard_map/all_to_all | solution.py:90
  41.3 90.7 %collective-permute-start = (f32[1,256]{1,0:T(1,128)S(1)}, f32[1,256]{1,0:T(1,128)S(1)}, u32[]{:S(2)}, u32[]{:S(2)}) collective-permute-start(f32[1,256]{1,0:T(1,128)S(1)} %slice.198), channel_id=1, source_target_pairs={{0,16},{16,32},{32,48},{48,64},{64,80},{80,96},{96,112},{112,128},... | collective-permute-start | bytes 3080 | tf_op jit(solution)/shard_map/ppermute | solution.py:15
  44.8 87.3 %collective-permute-start.1 = (f32[256,1]{1,0:T(8,128)S(1)}, f32[256,1]{1,0:T(8,128)S(1)}, u32[]{:S(2)}, u32[]{:S(2)}) collective-permute-start(f32[256,1]{1,0:T(8,128)S(1)} %slice.200), channel_id=1, source_target_pairs={{0,1},{1,2},{2,3},{3,4},{4,5},{5,6},{6,7},{7,8},{8,9},{9,10},{10,1... | collective-permute-start | bytes 3080 | tf_op jit(solution)/shard_map/ppermute | solution.py:15
  46.8 78.3 %collective-permute-start.2 = (f32[2,1,256]{2,1,0:T(1,128)S(1)}, f32[2,1,256]{2,1,0:T(1,128)S(1)}, u32[]{:S(2)}, u32[]{:S(2)}) collective-permute-start(f32[2,1,256]{2,1,0:T(1,128)S(1)} %slice.263), channel_id=1, source_target_pairs={{16,0},{32,16},{48,32},{64,48},{80,64},{96,80},{112,96},{128,112},... | collective-permute-start | bytes 6152 | tf_op jit(solution)/shard_map/ppermute | solution.py:15
  52.6 72.4 %collective-permute-start.3 = (f32[2,256,1]{2,1,0:T(8,128)S(1)}, f32[2,256,1]{2,1,0:T(8,128)S(1)}, u32[]{:S(2)}, u32[]{:S(2)}) collective-permute-start(f32[2,256,1]{2,1,0:T(8,128)S(1)} %slice.266), channel_id=1, source_target_pairs={{1,0},{2,1},{3,2},{4,3},{5,4},{6,5},{7,6},{8,7},{9,8},{10,9},{11,1... | collective-permute-start | bytes 6152 | tf_op jit(solution)/shard_map/ppermute | solution.py:15
  57.9 85.7 %copy-start.6 = (f32[256,256]{1,0:T(8,128)S(1)}, f32[256,256]{1,0:T(8,128)}, u32[]{:S(2)}) copy-start(f32[256,256]{1,0:T(8,128)} %param.11) | copy-start | bytes 786436
  57.9 85.7 %copy-start.7 = (bf16[2,256,256]{2,1,0:T(8,128)(2,1)S(1)}, bf16[2,256,256]{2,1,0:T(8,128)(2,1)}, u32[]{:S(2)}) copy-start(bf16[2,256,256]{2,1,0:T(8,128)(2,1)} %param.12) | copy-start | bytes 786436
  132.6 4.9 %collective-permute-start.5 = (f32[2,256]{1,0:T(2,128)S(1)}, f32[2,256]{1,0:T(2,128)S(1)}, u32[]{:S(2)}, u32[]{:S(2)}) collective-permute-start(f32[2,256]{1,0:T(2,128)S(1)} %pad_maximum_fusion.3), channel_id=1, source_target_pairs={{0,1},{1,2},{2,3},{3,4},{4,5},{5,6},{6,7},{7,8},{8,9},{9,10},{10,1... | collective-permute-start | bytes 6152 | tf_op jit(solution)/shard_map/ppermute | solution.py:15
  134.5 8.8 %collective-permute-start.4 = (f32[2,256]{1,0:T(2,128)S(1)}, f32[2,256]{1,0:T(2,128)S(1)}, u32[]{:S(2)}, u32[]{:S(2)}) collective-permute-start(f32[2,256]{1,0:T(2,128)S(1)} %pad_maximum_fusion.2), channel_id=1, source_target_pairs={{0,16},{16,32},{32,48},{48,64},{64,80},{80,96},{96,112},{112,128},... | collective-permute-start | bytes 6152 | tf_op jit(solution)/shard_map/ppermute | solution.py:15
  143.6 8.7 %copy-start.2 = (f32[1,256,256]{2,1,0:T(8,128)}, f32[1,256,256]{2,1,0:T(8,128)S(1)}, u32[]{:S(2)}) copy-start(f32[1,256,256]{2,1,0:T(8,128)S(1)} %get-tuple-element.29) | copy-start | bytes 786436
  143.6 8.7 %copy-start.3 = (f32[1,256,256]{2,1,0:T(8,128)}, f32[1,256,256]{2,1,0:T(8,128)S(1)}, u32[]{:S(2)}) copy-start(f32[1,256,256]{2,1,0:T(8,128)S(1)} %get-tuple-element.30) | copy-start | bytes 786436
  143.8 6.5 %collective-permute-start.6 = (f32[2,1,256]{2,1,0:T(1,128)S(1)}, f32[2,1,256]{2,1,0:T(1,128)S(1)}, u32[]{:S(2)}, u32[]{:S(2)}) collective-permute-start(f32[2,1,256]{2,1,0:T(1,128)S(1)} %slice.283), channel_id=1, source_target_pairs={{16,0},{32,16},{48,32},{64,48},{80,64},{96,80},{112,96},{128,112},... | collective-permute-start | bytes 6152 | tf_op jit(solution)/shard_map/ppermute | solution.py:15
  145.7 6.4 %collective-permute-start.7 = (f32[2,256,1]{2,1,0:T(8,128)S(1)}, f32[2,256,1]{2,1,0:T(8,128)S(1)}, u32[]{:S(2)}, u32[]{:S(2)}) collective-permute-start(f32[2,256,1]{2,1,0:T(8,128)S(1)} %slice.286), channel_id=1, source_target_pairs={{1,0},{2,1},{3,2},{4,3},{5,4},{6,5},{7,6},{8,7},{9,8},{10,9},{11,1... | collective-permute-start | bytes 6152 | tf_op jit(solution)/shard_map/ppermute | solution.py:15
  148.5 0.7 copy-start.4
  152.8 7.6 %collective-permute-start.9 = (f32[2,256]{1,0:T(2,128)S(1)}, f32[2,256]{1,0:T(2,128)S(1)}, u32[]{:S(2)}, u32[]{:S(2)}) collective-permute-start(f32[2,256]{1,0:T(2,128)S(1)} %pad_maximum_fusion.5), channel_id=1, source_target_pairs={{0,1},{1,2},{2,3},{3,4},{4,5},{5,6},{6,7},{7,8},{8,9},{9,10},{10,1... | collective-permute-start | bytes 6152 | tf_op jit(solution)/shard_map/ppermute | solution.py:15
  156.6 8.8 %collective-permute-start.8 = (f32[2,256]{1,0:T(2,128)S(1)}, f32[2,256]{1,0:T(2,128)S(1)}, u32[]{:S(2)}, u32[]{:S(2)}) collective-permute-start(f32[2,256]{1,0:T(2,128)S(1)} %pad_maximum_fusion.4), channel_id=1, source_target_pairs={{0,16},{16,32},{32,48},{48,64},{64,80},{80,96},{96,112},{112,128},... | collective-permute-start | bytes 6152 | tf_op jit(solution)/shard_map/ppermute | solution.py:15
  166.3 9.1 %copy-start.8 = (f32[1,256,256]{2,1,0:T(8,128)}, f32[1,256,256]{2,1,0:T(8,128)S(1)}, u32[]{:S(2)}) copy-start(f32[1,256,256]{2,1,0:T(8,128)S(1)} %get-tuple-element.24) | copy-start | bytes 786436
  177.5 5.5 %collective-permute-start.10 = (f32[2,1,256]{2,1,0:T(1,128)S(1)}, f32[2,1,256]{2,1,0:T(1,128)S(1)}, u32[]{:S(2)}, u32[]{:S(2)}) collective-permute-start(f32[2,1,256]{2,1,0:T(1,128)S(1)} %slice.303), channel_id=1, source_target_pairs={{16,0},{32,16},{48,32},{64,48},{80,64},{96,80},{112,96},{128,112},... | collective-permute-start | bytes 6152 | tf_op jit(solution)/shard_map/ppermute | solution.py:15
  179.5 5.8 %collective-permute-start.11 = (f32[2,256,1]{2,1,0:T(8,128)S(1)}, f32[2,256,1]{2,1,0:T(8,128)S(1)}, u32[]{:S(2)}, u32[]{:S(2)}) collective-permute-start(f32[2,256,1]{2,1,0:T(8,128)S(1)} %slice.306), channel_id=1, source_target_pairs={{1,0},{2,1},{3,2},{4,3},{5,4},{6,5},{7,6},{8,7},{9,8},{10,9},{11,1... | collective-permute-start | bytes 6152 | tf_op jit(solution)/shard_map/ppermute | solution.py:15
  185.5 18.5 %copy-start.5 = (f32[2,128,2,128]{3,2,1,0:T(2,128)S(1)}, f32[2,128,2,128]{3,2,1,0:T(2,128)}, u32[]{:S(2)}) copy-start(f32[2,128,2,128]{3,2,1,0:T(2,128)} %copy-done.4) | copy-start | bytes 786436
  185.9 10.1 %collective-permute-start.13 = (f32[2,256]{1,0:T(2,128)S(1)}, f32[2,256]{1,0:T(2,128)S(1)}, u32[]{:S(2)}, u32[]{:S(2)}) collective-permute-start(f32[2,256]{1,0:T(2,128)S(1)} %pad_maximum_fusion.7), channel_id=1, source_target_pairs={{0,1},{1,2},{2,3},{3,4},{4,5},{5,6},{6,7},{7,8},{8,9},{9,10},{10,1... | collective-permute-start | bytes 6152 | tf_op jit(solution)/shard_map/ppermute | solution.py:15
  192.1 8.8 %collective-permute-start.12 = (f32[2,256]{1,0:T(2,128)S(1)}, f32[2,256]{1,0:T(2,128)S(1)}, u32[]{:S(2)}, u32[]{:S(2)}) collective-permute-start(f32[2,256]{1,0:T(2,128)S(1)} %pad_maximum_fusion.6), channel_id=1, source_target_pairs={{0,16},{16,32},{32,48},{48,64},{64,80},{80,96},{96,112},{112,128},... | collective-permute-start | bytes 6152 | tf_op jit(solution)/shard_map/ppermute | solution.py:15
  197.0 7.1 %copy-start.9 = (f32[256,256]{1,0:T(8,128)S(1)}, f32[256,256]{1,0:T(8,128)}, u32[]{:S(2)}) copy-start(f32[256,256]{1,0:T(8,128)} %get-tuple-element.5) | copy-start | bytes 786436
where the time goes:
time: 206 us; the launch traced here: 205 us
  waiting for transfers between devices  96.6 us (47%)
  starting transfers between devices  72.8 us (35%)
  local copies, waits for them, and re-layouts  18.8 us (9%)
  other arithmetic  12.3 us (6%)
  matrix products  3.8 us (2%)
    ppermute x14, waiting for transfers between devices, from_behind(): lax.ppermute(value, axis, [(source, source + steps) for source in range(f...  94.6 us
    ppermute x14, starting transfers between devices, from_behind(): lax.ppermute(value, axis, [(source, source + steps) for source in range(f...  44.2 us
    unnamed x26, local copies, waits for them, and re-layouts  10.1 us
    all_to_all x1, starting transfers between devices, body(): lax.all_to_all(obs_buffer.reshape(places, 2, tile, tile), 'gx', split_axi...  9.9 us
    all_to_all x1, starting transfers between devices, body(): lax.all_to_all(weight_buffer, 'gx', split_axis=0, concat_axis=0, tiled=True)  9.86 us
    all_to_all x1, starting transfers between devices, body(): lax.all_to_all(slot_buffer, 'gx', split_axis=0, concat_axis=0, tiled=True)  8.81 us
  transfers between devices with their start and end apart: 17, of which 11 were waited for; matrix products, arithmetic and copies ran while one was open for 7% of the time, Pallas kernels for 0%

commit v1 on v0

v1 whole, which is shorter than its diff:
```python
import functools

import jax
import jax.numpy as jnp
from jax import lax
from jax.experimental import pallas as pl
from jax.experimental.pallas import tpu as pltpu
from jax.sharding import PartitionSpec as P

OMEGA = 0.6
NX, NZ = 4, 8
SLOTS = 4
ROWS = 16
LEAD = 2
GAP = 1
MESH = pl.DeviceIdType.MESH


def from_behind(value, axis, steps):
    count = lax.axis_size(axis)
    first, last = (max(0, -steps), min(count, count - steps))
    return lax.ppermute(value, axis, [(source, source + steps) for source in range(first, last)])


def exchange_kernel(
    meta_ref, obs_ref, out_ref, wsum_ref,
    meta, ag, table, part, part_w, rp1, rp, rm1, rm, rw,
    own_sem, meta_s, meta_r, ag_s, ag_r, rs_s, rs_r, rw_s, rw_r,
):
    chunks = ag.shape[1]
    scenes = ag.shape[2]
    half = scenes // 2
    me_x, me_y = lax.axis_index("gx"), lax.axis_index("gy")
    x, z = lax.rem(me_x, NX), me_x // NX
    x_right = (z * NX + lax.rem(x + 1, NX), me_y)
    x_left = (z * NX + lax.rem(x + NX - 1, NX), me_y)
    x_far = (z * NX + lax.rem(x + 2, NX), me_y)
    z_right = (lax.rem(z + 1, NZ) * NX + x, me_y)
    z_left = (lax.rem(z + NZ - 1, NZ) * NX + x, me_y)

    def remote(src, dst, send, recv, device):
        return pltpu.make_async_remote_copy(
            src_ref=src, dst_ref=dst, send_sem=send, recv_sem=recv, device_id=device, device_id_type=MESH
        )

    def rows(c):
        return pl.ds(pl.multiple_of(c * ROWS, ROWS), ROWS)

    def own_load(c):
        return pltpu.make_async_copy(obs_ref.at[:, rows(c), :], ag.at[0, c], own_sem.at[c])

    def own_send(side, c):
        return remote(
            obs_ref.at[:, rows(c), :], ag.at[1 + side, c], ag_s.at[side, c], ag_r.at[side, c],
            (x_right, x_left)[side],
        )

    def far_send(side, c):
        piece = pl.ds(side * half, half)
        return remote(
            ag.at[1 + side, c, piece], ag.at[3, c, piece], ag_s.at[2 + side, c], ag_r.at[2 + side, c],
            (x_right, x_left)[side],
        )

    def meta_send(peer):
        return remote(
            meta_ref, meta.at[peer], meta_s.at[peer], meta_r.at[peer], (x_right, x_left, x_far)[peer]
        )

    def ring_send(side, stage, c):
        device = (z_right, z_left)[side]
        semaphores = (rs_s.at[side * 4 + stage - 1, c], rs_r.at[side * 4 + stage - 1, c])
        if stage == 1:
            return remote(
                part.at[c, 4, pl.ds(side * 2, 2)], (rp1, rm1)[side].at[c], *semaphores, device
            )
        source = 5 - stage if side == 0 else 3 + stage
        return remote(part.at[c, source], (rp, rm)[side].at[stage - 2, c], *semaphores, device)

    def ring_send_w(side, stage):
        source = 5 - stage if side == 0 else (8 if stage == 1 else 3 + stage)
        index = side * 4 + stage - 1
        return remote(
            part_w.at[source], rw.at[index], rw_s.at[index], rw_r.at[index], (z_right, z_left)[side]
        )

    barrier = pltpu.get_barrier_semaphore()
    for device in (x_right, x_left, x_far, z_right, z_left):
        pl.semaphore_signal(barrier, inc=1, device_id=device, device_id_type=MESH)
    for c in range(chunks):
        own_load(c).start()
    pl.semaphore_wait(barrier, 5)

    for peer in range(3):
        meta_send(peer).start()
    for c in range(LEAD):
        own_send(0, c).start()
        own_send(1, c).start()

    width = scenes * ROWS
    count = NZ * SLOTS * ROWS

    def fill(source, block):
        key, weight = block[0:1, :], block[1:2, :]
        row = lax.broadcasted_iota(jnp.int32, (count, 1), 0)
        lane = lax.broadcasted_iota(jnp.int32, (1, width), 1)
        target_z = lax.rem(z + row // (SLOTS * ROWS), NZ)
        want = (target_z * NX + x) * SLOTS + lax.rem(row // ROWS, SLOTS)
        want = want.astype(jnp.float32)
        hit = jnp.logical_and(key == want, lax.rem(lane, ROWS) == lax.rem(row, ROWS))
        table[:, source * width : (source + 1) * width] = jnp.where(hit, weight, 0.0).astype(jnp.bfloat16)
        row = lax.broadcasted_iota(jnp.int32, (NZ * 8, 1), 0)
        slot = lax.rem(row, 8)
        target_z = lax.rem(z + row // 8, NZ)
        want = jnp.where(slot < SLOTS, (target_z * NX + x) * SLOTS + slot, -1).astype(jnp.float32)
        hit = jnp.logical_and(key == want, lax.rem(lane, ROWS) == 0)
        return jnp.sum(jnp.where(hit, weight, 0.0), axis=1, keepdims=True)

    total_w = fill(0, meta_ref[...])
    for peer in range(3):
        meta_send(peer).wait_recv()
        total_w = total_w + fill(1 + peer, meta[peer])
    total_w = jnp.broadcast_to(total_w, (NZ * 8, 128)).reshape(NZ, 8, 128)
    part_w[0:NZ] = total_w
    slot = lax.broadcasted_iota(jnp.int32, (8, 128), 0)
    part_w[4] = jnp.where(slot < 2, total_w[4], 0.0)
    part_w[8] = jnp.where(slot < 2, 0.0, total_w[4])
    ring_send_w(0, 1).start()
    ring_send_w(1, 1).start()
    for c in range(chunks):
        own_load(c).wait()

    def at_chunk(c, action):
        pl.when(jnp.logical_and(c >= 0, c < chunks))(lambda: action(c))

    def combine(c):
        for side in range(2):
            far_send(side, c).wait_recv()
        columns = []
        for h in range(ROWS // 16):
            columns.append(
                jnp.concatenate(
                    [ag[s, c, :, h * 16 : (h + 1) * 16, :].reshape(scenes * 16, 128) for s in range(4)], axis=0
                )
            )
        stacked = columns[0] if len(columns) == 1 else jnp.concatenate(columns, axis=1)
        sums = jnp.dot(table[...], stacked, preferred_element_type=jnp.float32)
        part[c] = sums.reshape(NZ, SLOTS, ROWS, 128)
        ring_send(0, 1, c).start()
        ring_send(1, 1, c).start()

    def ring_step(stage, c):
        for side in range(2):
            ring_send(side, stage - 1, c).wait_recv()
            mine = 5 - stage if side == 0 else 3 + stage
            if stage == 2:
                part[c, mine, side * 2 : side * 2 + 2] += (rp1, rm1)[side][c]
            else:
                part[c, mine] += (rp, rm)[side][stage - 3, c]
            ring_send(side, stage, c).start()

    def finish(c):
        for side in range(2):
            ring_send(side, 4, c).wait_recv()
        out_ref[:, rows(c), :] = part[c, 0] + (rp[2, c] + rm[2, c])

    def ring_step_w(stage):
        for side in range(2):
            ring_send_w(side, stage - 1).wait_recv()
            mine = 5 - stage if side == 0 else 3 + stage
            part_w[mine] += rw[side * 4 + stage - 2]
            ring_send_w(side, stage).start()

    def step(k, carry):
        @pl.when(k + LEAD < chunks)
        def _():
            own_send(0, k + LEAD).start()
            own_send(1, k + LEAD).start()

        @pl.when(k < chunks)
        def _():
            for side in range(2):
                own_send(side, k).wait_recv()
                far_send(side, k).start()

        at_chunk(k - 1 - 4 * GAP, finish)
        for stage in (4, 3, 2):
            at_chunk(k - 1 - (stage - 1) * GAP, functools.partial(ring_step, stage))
            pl.when(k == stage + 1)(functools.partial(ring_step_w, stage))
        at_chunk(k - 1, combine)
        return carry

    lax.fori_loop(0, chunks + 1 + 4 * GAP, step, 0)
    for side in range(2):
        ring_send_w(side, 4).wait_recv()
    wsum_ref[...] = part_w[0] + (rw[3] + rw[7])

    def drain(c, carry):
        for side in range(2):
            own_send(side, c).wait_send()
            far_send(side, c).wait_send()
            for stage in range(1, 5):
                ring_send(side, stage, c).wait_send()
        return carry

    lax.fori_loop(0, chunks, drain, 0)
    for peer in range(3):
        meta_send(peer).wait_send()
    for side in range(2):
        for stage in range(1, 5):
            ring_send_w(side, stage).wait_send()


def exchange(obs, owners, slots, weights):
    scenes, _, tile, _ = obs.shape
    height = 2 * tile
    chunks = height // ROWS
    key = jnp.repeat((owners * SLOTS + slots).astype(jnp.float32), ROWS)
    weight = jnp.repeat(weights.astype(jnp.float32), ROWS)
    meta = jnp.concatenate([key[None], weight[None], jnp.zeros((6, scenes * ROWS), jnp.float32)], axis=0)
    f32, bf16 = jnp.float32, jnp.bfloat16
    dma = pltpu.SemaphoreType.DMA
    return pl.pallas_call(
        exchange_kernel,
        out_shape=(
            jax.ShapeDtypeStruct((SLOTS, height, tile), f32),
            jax.ShapeDtypeStruct((8, 128), f32),
        ),
        in_specs=[pl.BlockSpec(memory_space=pltpu.VMEM), pl.BlockSpec(memory_space=pl.ANY)],
        out_specs=(pl.BlockSpec(memory_space=pltpu.VMEM), pl.BlockSpec(memory_space=pltpu.VMEM)),
        scratch_shapes=[
            pltpu.VMEM((3, 8, scenes * ROWS), f32),
            pltpu.VMEM((4, chunks, scenes, ROWS, tile), bf16),
            pltpu.VMEM((NZ * SLOTS * ROWS, 4 * scenes * ROWS), bf16),
            pltpu.VMEM((chunks, NZ, SLOTS, ROWS, tile), f32),
            pltpu.VMEM((NZ + 1, 8, 128), f32),
            pltpu.VMEM((chunks, 2, ROWS, tile), f32),
            pltpu.VMEM((3, chunks, SLOTS, ROWS, tile), f32),
            pltpu.VMEM((chunks, 2, ROWS, tile), f32),
            pltpu.VMEM((3, chunks, SLOTS, ROWS, tile), f32),
            pltpu.VMEM((8, 8, 128), f32),
            dma((chunks,)),
            dma((3,)), dma((3,)),
            dma((4, chunks)), dma((4, chunks)),
            dma((8, chunks)), dma((8, chunks)),
            dma((8,)), dma((8,)),
        ],
        compiler_params=pltpu.CompilerParams(
            collective_id=0, has_side_effects=True, vmem_limit_bytes=48 * 1024 * 1024
        ),
    )(meta, obs.reshape(scenes, height, tile))


def stress_image(field, visc):
    above_x = from_behind(field[:, :1, :], "gx", -1)
    above_y = from_behind(field[:, :, :1], "gy", -1)
    along_x = jnp.concatenate([field[:, 1:, :], above_x], axis=1) - field
    along_y = jnp.concatenate([field[:, :, 1:], above_y], axis=2) - field
    sxx = visc * (4.0 * along_x[0] + 2.0 * along_y[1])
    syy = visc * (4.0 * along_y[1] + 2.0 * along_x[0])
    sxy = visc * (along_y[0] + along_x[1])
    below_x = from_behind(jnp.stack([sxx[-1], sxy[-1]]), "gx", 1)
    below_y = from_behind(jnp.stack([sxy[:, -1], syy[:, -1]]), "gy", 1)
    push_u = (
        jnp.concatenate([below_x[0:1], sxx[:-1]], axis=0)
        - sxx
        + jnp.concatenate([below_y[0][:, None], sxy[:, :-1]], axis=1)
        - sxy
    )
    push_v = (
        jnp.concatenate([below_x[1:2], sxy[:-1]], axis=0)
        - sxy
        + jnp.concatenate([below_y[1][:, None], syy[:, :-1]], axis=1)
        - syy
    )
    return jnp.stack([push_u, push_v])


def spread_tiles(values, tiles_x, tiles_y, tile):
    wide = jnp.broadcast_to(values.reshape(tiles_x, 1, tiles_y, 1), (tiles_x, tile, tiles_y, tile))
    return wide.reshape(tiles_x * tile, tiles_y * tile)


def body(vel0, visc, fric, drive, scene_obs, scene_weight, scene_owner, scene_slot, ice_mask):
    cells_x, cells_y = visc.shape
    tile = scene_obs.shape[-1]
    tiles_x = cells_x // tile
    tiles_y = cells_y // tile
    summed, tile_weight = exchange(scene_obs[0], scene_owner[0, :, 0], scene_slot[0], scene_weight[0])
    visc_row = from_behind(visc[-1:, :], "gx", 1)
    visc_col = from_behind(visc[:, -1:], "gy", 1)
    visc_x = jnp.concatenate([visc_row, visc[:-1]], axis=0)
    visc_y = jnp.concatenate([visc_col, visc[:, :-1]], axis=1)
    diag = jnp.stack([5.0 * visc + 4.0 * visc_x + visc_y, 5.0 * visc + visc_x + 4.0 * visc_y])
    relax = 1.0 / (diag + fric)
    start = vel0.astype(jnp.float32)
    force = drive.astype(jnp.float32)
    first_res = force - stress_image(start, visc) - fric * start
    first = start + OMEGA * relax * first_res
    second_res = force - stress_image(first, visc) - fric * first
    second = first + OMEGA * relax * second_res
    obs_sum = (
        summed.reshape(tiles_x, tiles_y, 2, tile, tile)
        .transpose(2, 0, 3, 1, 4)
        .reshape(2, cells_x, cells_y)
    )
    weight_cell = spread_tiles(tile_weight[:SLOTS, 0], tiles_x, tiles_y, tile)
    ice = spread_tiles(ice_mask.astype(jnp.float32), tiles_x, tiles_y, tile)
    misfit_grad = ice * (weight_cell * second - obs_sum)
    lift_two = OMEGA * relax * misfit_grad
    back = misfit_grad - stress_image(lift_two, visc) - fric * lift_two
    lift_one = OMEGA * relax * back
    part_one = jnp.sum(lift_one * (relax * first_res + start), axis=0)
    part_two = jnp.sum(lift_two * (relax * second_res + first), axis=0)
    return -ice * (part_one + part_two)


def solution(mesh):
    placed = (
        P(None, "gx", "gy"),
        P("gx", "gy"),
        P("gx", "gy"),
        P(None, "gx", "gy"),
        P("gy", "gx", None, None, None),
        P("gy", "gx"),
        P("gy", "gx", None),
        P("gy", "gx"),
        P("gx", "gy"),
    )
    return jax.shard_map(body, mesh=mesh, in_specs=placed, out_specs=P("gx", "gy"), check_vma=False)
```

time: 206 us -> 177 us (0.86)
  the two profiles are of different devices: /device:TPU:272 before, /device:TPU:88 now
where the time goes in v1:
time: 177 us
  Pallas kernels  94.1 us (53%)
  starting transfers between devices  45.1 us (25%)
  waiting for transfers between devices  17.6 us (10%)
  local copies, waits for them, and re-layouts  14 us (8%)
  other arithmetic  5.07 us (3%)
    pallas_call x1, Pallas kernels, exchange(): pl.pallas_call(exchange_kernel, out_shape=(jax.ShapeDtypeStruct((SLOTS, h...  94.1 us
    ppermute x14, starting transfers between devices, from_behind(): lax.ppermute(value, axis, [(source, source + steps) for source in range(f...  45.1 us
    ppermute x14, waiting for transfers between devices, from_behind(): lax.ppermute(value, axis, [(source, source + steps) for source in range(f...  17.6 us
    unnamed x52, local copies, waits for them, and re-layouts  5.17 us
  transfers between devices with their start and end apart: 14, of which 6 were waited for; matrix products, arithmetic and copies ran while one was open for 4% of the time, Pallas kernels for 53%

profile of v1, /device:TPU:88, one launch (start us, length us, event | category | flops | bytes accessed | tf_op | source)
XLA Modules:
  0.0 176.6 jit_solution(14186000828306911758)
XLA Ops:
  0.0 0.7 slice.201
  0.7 3.4 %collective-permute-start = (f32[1,256]{1,0:T(1,128)S(1)}, f32[1,256]{1,0:T(1,128)S(1)}, u32[]{:S(2)}, u32[]{:S(2)}) collective-permute-start(f32[1,256]{1,0:T(1,128)S(1)} %slice.201), channel_id=1, source_target_pairs={{0,16},{16,32},{32,48},{48,64},{64,80},{80,96},{96,112},{112,128},... | collective-permute-start | bytes 3080 | tf_op jit(solution)/shard_map/ppermute | solution.py:22
  4.1 0.7 slice.267
  4.8 4.5 %collective-permute-start.2 = (f32[2,1,256]{2,1,0:T(1,128)S(1)}, f32[2,1,256]{2,1,0:T(1,128)S(1)}, u32[]{:S(2)}, u32[]{:S(2)}) collective-permute-start(f32[2,1,256]{2,1,0:T(1,128)S(1)} %slice.267), channel_id=1, source_target_pairs={{16,0},{32,16},{48,32},{64,48},{80,64},{96,80},{112,96},{128,112},... | collective-permute-start | bytes 6152 | tf_op jit(solution)/shard_map/ppermute | solution.py:22
  9.4 1.0 slice.203
  10.4 1.9 %collective-permute-start.1 = (f32[256,1]{1,0:T(8,128)S(1)}, f32[256,1]{1,0:T(8,128)S(1)}, u32[]{:S(2)}, u32[]{:S(2)}) collective-permute-start(f32[256,1]{1,0:T(8,128)S(1)} %slice.203), channel_id=1, source_target_pairs={{0,1},{1,2},{2,3},{3,4},{4,5},{5,6},{6,7},{7,8},{8,9},{9,10},{10,1... | collective-permute-start | bytes 3080 | tf_op jit(solution)/shard_map/ppermute | solution.py:22
  12.4 3.6 %collective-permute-start.3 = (f32[2,256,1]{2,1,0:T(8,128)S(1)}, f32[2,256,1]{2,1,0:T(8,128)S(1)}, u32[]{:S(2)}, u32[]{:S(2)}) collective-permute-start(f32[2,256,1]{2,1,0:T(8,128)S(1)} %slice.270), channel_id=1, source_target_pairs={{1,0},{2,1},{3,2},{4,3},{5,4},{6,5},{7,6},{8,7},{9,8},{10,9},{11,1... | collective-permute-start | bytes 6152 | tf_op jit(solution)/shard_map/ppermute | solution.py:22
  16.6 1.2 copy-done
  17.8 94.1 %shard_map.91 = (f32[4,256,128]{2,1,0:T(8,128)S(1)}, f32[8,128]{1,0:T(8,128)S(1)}) custom-call(f32[8,256]{1,0:T(8,128)S(1)} %maximum_maximum_fusion.meta_ref, bf16[16,256,128]{2,1,0:T(8,128)(2,1)S(1)} %bitcast.95), custom_call_target="tpu_custom_call" | custom-call | tf_op jit(solution)/shard_map/pallas_call | solution.py:223
  111.9 0.1 slice_reduce_fusion.6
  112.1 0.1 slice.269
  112.3 0.6 copy-done.22
  113.0 0.1 convert_subtract_fusion.3
  113.2 0.8 copy-done.2
  113.9 0.2 add_bitcast_fusion.1
  114.2 0.2 slice_reduce_fusion.4
  114.4 1.9 %collective-permute-start.5 = (f32[2,256]{1,0:T(2,128)S(1)}, f32[2,256]{1,0:T(2,128)S(1)}, u32[]{:S(2)}, u32[]{:S(2)}) collective-permute-start(f32[2,256]{1,0:T(2,128)S(1)} %pad_maximum_fusion.3), channel_id=1, source_target_pairs={{0,1},{1,2},{2,3},{3,4},{4,5},{5,6},{6,7},{7,8},{8,9},{9,10},{10,1... | collective-permute-start | bytes 6152 | tf_op jit(solution)/shard_map/ppermute | solution.py:22
  116.4 3.3 %collective-permute-start.4 = (f32[2,256]{1,0:T(2,128)S(1)}, f32[2,256]{1,0:T(2,128)S(1)}, u32[]{:S(2)}, u32[]{:S(2)}) collective-permute-start(f32[2,256]{1,0:T(2,128)S(1)} %pad_maximum_fusion.2), channel_id=1, source_target_pairs={{0,16},{16,32},{32,48},{48,64},{64,80},{80,96},{96,112},{112,128},... | collective-permute-start | bytes 6152 | tf_op jit(solution)/shard_map/ppermute | solution.py:22
  119.6 0.1 copy.11
  119.8 0.1 copy.12
  119.9 4.0 %collective-permute-done.4 = f32[2,256]{1,0:T(2,128)S(1)} collective-permute-done((f32[2,256]{1,0:T(2,128)S(1)}, f32[2,256]{1,0:T(2,128)S(1)}, u32[]{:S(2)}, u32[]{:S(2)}) %collective-permute-start.4) | collective-permute-done | bytes 2080 | tf_op jit(solution)/shard_map/ppermute | solution.py:22
  124.0 0.2 fusion.16
  124.2 0.7 copy-done.9
  125.0 0.2 convert_add_fusion.1
  125.2 0.7 slice.290
  125.9 3.2 %collective-permute-start.6 = (f32[2,1,256]{2,1,0:T(1,128)S(1)}, f32[2,1,256]{2,1,0:T(1,128)S(1)}, u32[]{:S(2)}, u32[]{:S(2)}) collective-permute-start(f32[2,1,256]{2,1,0:T(1,128)S(1)} %slice.287), channel_id=1, source_target_pairs={{16,0},{32,16},{48,32},{64,48},{80,64},{96,80},{112,96},{128,112},... | collective-permute-start | bytes 6152 | tf_op jit(solution)/shard_map/ppermute | solution.py:22
  129.1 2.2 %collective-permute-start.7 = (f32[2,256,1]{2,1,0:T(8,128)}, f32[2,256,1]{2,1,0:T(8,128)S(1)}, u32[]{:S(2)}, u32[]{:S(2)}) collective-permute-start(f32[2,256,1]{2,1,0:T(8,128)} %slice.290), channel_id=1, source_target_pairs={{1,0},{2,1},{3,2},{4,3},{5,4},{6,5},{7,6},{8,7},{9,8},{10,9},{11,1... | collective-permute-start | bytes 6152 | tf_op jit(solution)/shard_map/ppermute | solution.py:22
  131.4 0.1 broadcast_in_dim.12
  131.5 0.1 broadcast_in_dim.30
  131.6 0.8 copy_bitcast_fusion
  132.5 0.4 copy.15
  132.9 0.4 reshape.54
  133.3 0.2 slice.289
  133.6 2.0 %collective-permute-done.7 = f32[2,256,1]{2,1,0:T(8,128)S(1)} collective-permute-done((f32[2,256,1]{2,1,0:T(8,128)}, f32[2,256,1]{2,1,0:T(8,128)S(1)}, u32[]{:S(2)}, u32[]{:S(2)}) %collective-permute-start.7) | collective-permute-done | bytes 2080 | tf_op jit(solution)/shard_map/ppermute | solution.py:22
  135.5 0.2 maximum_subtract_fusion
  135.7 0.1 bitcast_multiply_fusion.3
  135.8 0.2 slice_reduce_fusion.3
  136.0 0.2 slice_reduce_fusion.2
  136.2 7.3 %collective-permute-start.9 = (f32[2,256]{1,0:T(2,128)S(1)}, f32[2,256]{1,0:T(2,128)S(1)}, u32[]{:S(2)}, u32[]{:S(2)}) collective-permute-start(f32[2,256]{1,0:T(2,128)S(1)} %pad_maximum_fusion.5), channel_id=1, source_target_pairs={{0,1},{1,2},{2,3},{3,4},{4,5},{5,6},{6,7},{7,8},{8,9},{9,10},{10,1... | collective-permute-start | bytes 6152 | tf_op jit(solution)/shard_map/ppermute | solution.py:22
  143.5 2.3 %collective-permute-start.8 = (f32[2,256]{1,0:T(2,128)S(1)}, f32[2,256]{1,0:T(2,128)S(1)}, u32[]{:S(2)}, u32[]{:S(2)}) collective-permute-start(f32[2,256]{1,0:T(2,128)S(1)} %pad_maximum_fusion.4), channel_id=1, source_target_pairs={{0,16},{16,32},{32,48},{48,64},{64,80},{80,96},{96,112},{112,128},... | collective-permute-start | bytes 6152 | tf_op jit(solution)/shard_map/ppermute | solution.py:22
  145.8 0.1 copy.13
  146.0 0.8 copy.14
  146.8 4.3 %collective-permute-done.8 = f32[2,256]{1,0:T(2,128)S(1)} collective-permute-done((f32[2,256]{1,0:T(2,128)S(1)}, f32[2,256]{1,0:T(2,128)S(1)}, u32[]{:S(2)}, u32[]{:S(2)}) %collective-permute-start.8) | collective-permute-done | bytes 2080 | tf_op jit(solution)/shard_map/ppermute | solution.py:22
  151.1 1.2 fusion.22
  152.3 1.0 multiply_reduce_fusion
  153.4 1.9 %collective-permute-start.10 = (f32[2,1,256]{2,1,0:T(1,128)S(1)}, f32[2,1,256]{2,1,0:T(1,128)S(1)}, u32[]{:S(2)}, u32[]{:S(2)}) collective-permute-start(f32[2,1,256]{2,1,0:T(1,128)S(1)} %slice.307), channel_id=1, source_target_pairs={{16,0},{32,16},{48,32},{64,48},{80,64},{96,80},{112,96},{128,112},... | collective-permute-start | bytes 6152 | tf_op jit(solution)/shard_map/ppermute | solution.py:22
  155.3 1.9 %collective-permute-start.11 = (f32[2,256,1]{2,1,0:T(8,128)S(1)}, f32[2,256,1]{2,1,0:T(8,128)S(1)}, u32[]{:S(2)}, u32[]{:S(2)}) collective-permute-start(f32[2,256,1]{2,1,0:T(8,128)S(1)} %slice.310), channel_id=1, source_target_pairs={{1,0},{2,1},{3,2},{4,3},{5,4},{6,5},{7,6},{8,7},{9,8},{10,9},{11,1... | collective-permute-start | bytes 6152 | tf_op jit(solution)/shard_map/ppermute | solution.py:22
  157.2 0.2 slice.309
  157.5 1.4 collective-permute-done.10
  158.8 2.2 %collective-permute-done.11 = f32[2,256,1]{2,1,0:T(8,128)S(1)} collective-permute-done((f32[2,256,1]{2,1,0:T(8,128)S(1)}, f32[2,256,1]{2,1,0:T(8,128)S(1)}, u32[]{:S(2)}, u32[]{:S(2)}) %collective-permute-start.11) | collective-permute-done | bytes 2080 | tf_op jit(solution)/shard_map/ppermute | solution.py:22
  161.1 0.1 maximum_subtract_fusion.2
  161.3 0.1 bitcast_multiply_fusion.1
  161.4 0.2 slice_reduce_fusion.1
  161.6 0.2 slice_reduce_fusion
  161.7 3.9 %collective-permute-start.13 = (f32[2,256]{1,0:T(2,128)S(1)}, f32[2,256]{1,0:T(2,128)S(1)}, u32[]{:S(2)}, u32[]{:S(2)}) collective-permute-start(f32[2,256]{1,0:T(2,128)S(1)} %pad_maximum_fusion.7), channel_id=1, source_target_pairs={{0,1},{1,2},{2,3},{3,4},{4,5},{5,6},{6,7},{7,8},{8,9},{9,10},{10,1... | collective-permute-start | bytes 6152 | tf_op jit(solution)/shard_map/ppermute | solution.py:22
  165.7 3.6 %collective-permute-start.12 = (f32[2,256]{1,0:T(2,128)S(1)}, f32[2,256]{1,0:T(2,128)S(1)}, u32[]{:S(2)}, u32[]{:S(2)}) collective-permute-start(f32[2,256]{1,0:T(2,128)S(1)} %pad_maximum_fusion.6), channel_id=1, source_target_pairs={{0,16},{16,32},{32,48},{48,64},{64,80},{80,96},{96,112},{112,128},... | collective-permute-start | bytes 6152 | tf_op jit(solution)/shard_map/ppermute | solution.py:22
  169.3 0.1 copy.16
  169.5 0.1 copy.17
  169.6 3.6 %collective-permute-done.12 = f32[2,256]{1,0:T(2,128)S(1)} collective-permute-done((f32[2,256]{1,0:T(2,128)S(1)}, f32[2,256]{1,0:T(2,128)S(1)}, u32[]{:S(2)}, u32[]{:S(2)}) %collective-permute-start.12) | collective-permute-done | bytes 2080 | tf_op jit(solution)/shard_map/ppermute | solution.py:22
  173.3 0.2 fusion.28
  173.6 0.6 copy-done.4
  174.8 0.5 fusion.2
  175.3 0.4 copy-done.8
  175.8 0.8 add_multiply_fusion
  (90 shorter events, 1.7 us)
Async XLA Ops:
  0.0 12.3 %copy-start.1 = (bf16[2,256,256]{2,1,0:T(8,128)(2,1)S(1)}, bf16[2,256,256]{2,1,0:T(8,128)(2,1)}, u32[]{:S(2)}) copy-start(bf16[2,256,256]{2,1,0:T(8,128)(2,1)} %param.9) | copy-start | bytes 786436
  0.7 112.4 %collective-permute-start = (f32[1,256]{1,0:T(1,128)S(1)}, f32[1,256]{1,0:T(1,128)S(1)}, u32[]{:S(2)}, u32[]{:S(2)}) collective-permute-start(f32[1,256]{1,0:T(1,128)S(1)} %slice.201), channel_id=1, source_target_pairs={{0,16},{16,32},{32,48},{48,64},{64,80},{80,96},{96,112},{112,128},... | collective-permute-start | bytes 3080 | tf_op jit(solution)/shard_map/ppermute | solution.py:22
  4.8 108.1 %collective-permute-start.2 = (f32[2,1,256]{2,1,0:T(1,128)S(1)}, f32[2,1,256]{2,1,0:T(1,128)S(1)}, u32[]{:S(2)}, u32[]{:S(2)}) collective-permute-start(f32[2,1,256]{2,1,0:T(1,128)S(1)} %slice.267), channel_id=1, source_target_pairs={{16,0},{32,16},{48,32},{64,48},{80,64},{96,80},{112,96},{128,112},... | collective-permute-start | bytes 6152 | tf_op jit(solution)/shard_map/ppermute | solution.py:22
  10.4 5.7 %copy-start.23 = (bf16[1,16]{1,0:T(2,128)(2,1)S(1)}, bf16[1,16]{1,0:T(2,128)(2,1)}, u32[]{:S(2)}) copy-start(bf16[1,16]{1,0:T(2,128)(2,1)} %param.14) | copy-start | bytes 100
  10.4 102.7 %collective-permute-start.1 = (f32[256,1]{1,0:T(8,128)S(1)}, f32[256,1]{1,0:T(8,128)S(1)}, u32[]{:S(2)}, u32[]{:S(2)}) collective-permute-start(f32[256,1]{1,0:T(8,128)S(1)} %slice.203), channel_id=1, source_target_pairs={{0,1},{1,2},{2,3},{3,4},{4,5},{5,6},{6,7},{7,8},{8,9},{9,10},{10,1... | collective-permute-start | bytes 3080 | tf_op jit(solution)/shard_map/ppermute | solution.py:22
  12.4 3.7 %copy-start.24 = (s32[1,16]{1,0:T(1,128)S(1)}, s32[1,16]{1,0:T(1,128)}, u32[]{:S(2)}) copy-start(s32[1,16]{1,0:T(1,128)} %param.16) | copy-start | bytes 196
  12.4 3.7 %copy-start.25 = (s32[1,16,1]{1,2,0:T(1,128)S(1)}, s32[1,16,1]{1,2,0:T(1,128)}, u32[]{:S(2)}) copy-start(s32[1,16,1]{1,2,0:T(1,128)} %param.15) | copy-start | bytes 196
  12.4 100.6 %collective-permute-start.3 = (f32[2,256,1]{2,1,0:T(8,128)S(1)}, f32[2,256,1]{2,1,0:T(8,128)S(1)}, u32[]{:S(2)}, u32[]{:S(2)}) collective-permute-start(f32[2,256,1]{2,1,0:T(8,128)S(1)} %slice.270), channel_id=1, source_target_pairs={{1,0},{2,1},{3,2},{4,3},{5,4},{6,5},{7,6},{8,7},{9,8},{10,9},{11,1... | collective-permute-start | bytes 6152 | tf_op jit(solution)/shard_map/ppermute | solution.py:22
  16.6 1.2 copy-start
  112.2 0.7 copy-start.22
  113.0 0.9 copy-start.2
  114.4 5.2 %collective-permute-start.5 = (f32[2,256]{1,0:T(2,128)S(1)}, f32[2,256]{1,0:T(2,128)S(1)}, u32[]{:S(2)}, u32[]{:S(2)}) collective-permute-start(f32[2,256]{1,0:T(2,128)S(1)} %pad_maximum_fusion.3), channel_id=1, source_target_pairs={{0,1},{1,2},{2,3},{3,4},{4,5},{5,6},{6,7},{7,8},{8,9},{9,10},{10,1... | collective-permute-start | bytes 6152 | tf_op jit(solution)/shard_map/ppermute | solution.py:22
  116.4 7.6 %collective-permute-start.4 = (f32[2,256]{1,0:T(2,128)S(1)}, f32[2,256]{1,0:T(2,128)S(1)}, u32[]{:S(2)}, u32[]{:S(2)}) collective-permute-start(f32[2,256]{1,0:T(2,128)S(1)} %pad_maximum_fusion.2), channel_id=1, source_target_pairs={{0,16},{16,32},{32,48},{48,64},{64,80},{80,96},{96,112},{112,128},... | collective-permute-start | bytes 6152 | tf_op jit(solution)/shard_map/ppermute | solution.py:22
  124.0 1.0 copy-start.9
  124.0 1.0 copy-start.11
  124.2 1.0 copy-start.3
  124.2 1.0 copy-start.5
  125.9 7.7 %collective-permute-start.6 = (f32[2,1,256]{2,1,0:T(1,128)S(1)}, f32[2,1,256]{2,1,0:T(1,128)S(1)}, u32[]{:S(2)}, u32[]{:S(2)}) collective-permute-start(f32[2,1,256]{2,1,0:T(1,128)S(1)} %slice.287), channel_id=1, source_target_pairs={{16,0},{32,16},{48,32},{64,48},{80,64},{96,80},{112,96},{128,112},... | collective-permute-start | bytes 6152 | tf_op jit(solution)/shard_map/ppermute | solution.py:22
  129.1 6.4 %collective-permute-start.7 = (f32[2,256,1]{2,1,0:T(8,128)}, f32[2,256,1]{2,1,0:T(8,128)S(1)}, u32[]{:S(2)}, u32[]{:S(2)}) collective-permute-start(f32[2,256,1]{2,1,0:T(8,128)} %slice.290), channel_id=1, source_target_pairs={{1,0},{2,1},{3,2},{4,3},{5,4},{6,5},{7,6},{8,7},{9,8},{10,9},{11,1... | collective-permute-start | bytes 6152 | tf_op jit(solution)/shard_map/ppermute | solution.py:22
  131.5 1.0 copy-start.7
  136.2 9.6 %collective-permute-start.9 = (f32[2,256]{1,0:T(2,128)S(1)}, f32[2,256]{1,0:T(2,128)S(1)}, u32[]{:S(2)}, u32[]{:S(2)}) collective-permute-start(f32[2,256]{1,0:T(2,128)S(1)} %pad_maximum_fusion.5), channel_id=1, source_target_pairs={{0,1},{1,2},{2,3},{3,4},{4,5},{5,6},{6,7},{7,8},{8,9},{9,10},{10,1... | collective-permute-start | bytes 6152 | tf_op jit(solution)/shard_map/ppermute | solution.py:22
  143.5 7.6 %collective-permute-start.8 = (f32[2,256]{1,0:T(2,128)S(1)}, f32[2,256]{1,0:T(2,128)S(1)}, u32[]{:S(2)}, u32[]{:S(2)}) collective-permute-start(f32[2,256]{1,0:T(2,128)S(1)} %pad_maximum_fusion.4), channel_id=1, source_target_pairs={{0,16},{16,32},{32,48},{48,64},{64,80},{80,96},{96,112},{112,128},... | collective-permute-start | bytes 6152 | tf_op jit(solution)/shard_map/ppermute | solution.py:22
  151.1 1.2 copy-start.17
  151.1 1.2 copy-start.19
  152.3 1.1 copy-start.13
  152.3 1.1 copy-start.15
  153.4 5.5 %collective-permute-start.10 = (f32[2,1,256]{2,1,0:T(1,128)S(1)}, f32[2,1,256]{2,1,0:T(1,128)S(1)}, u32[]{:S(2)}, u32[]{:S(2)}) collective-permute-start(f32[2,1,256]{2,1,0:T(1,128)S(1)} %slice.307), channel_id=1, source_target_pairs={{16,0},{32,16},{48,32},{64,48},{80,64},{96,80},{112,96},{128,112},... | collective-permute-start | bytes 6152 | tf_op jit(solution)/shard_map/ppermute | solution.py:22
  155.3 5.8 %collective-permute-start.11 = (f32[2,256,1]{2,1,0:T(8,128)S(1)}, f32[2,256,1]{2,1,0:T(8,128)S(1)}, u32[]{:S(2)}, u32[]{:S(2)}) collective-permute-start(f32[2,256,1]{2,1,0:T(8,128)S(1)} %slice.310), channel_id=1, source_target_pairs={{1,0},{2,1},{3,2},{4,3},{5,4},{6,5},{7,6},{8,7},{9,8},{10,9},{11,1... | collective-permute-start | bytes 6152 | tf_op jit(solution)/shard_map/ppermute | solution.py:22
  161.7 7.6 %collective-permute-start.13 = (f32[2,256]{1,0:T(2,128)S(1)}, f32[2,256]{1,0:T(2,128)S(1)}, u32[]{:S(2)}, u32[]{:S(2)}) collective-permute-start(f32[2,256]{1,0:T(2,128)S(1)} %pad_maximum_fusion.7), channel_id=1, source_target_pairs={{0,1},{1,2},{2,3},{3,4},{4,5},{5,6},{6,7},{7,8},{8,9},{9,10},{10,1... | collective-permute-start | bytes 6152 | tf_op jit(solution)/shard_map/ppermute | solution.py:22
  165.7 7.6 %collective-permute-start.12 = (f32[2,256]{1,0:T(2,128)S(1)}, f32[2,256]{1,0:T(2,128)S(1)}, u32[]{:S(2)}, u32[]{:S(2)}) collective-permute-start(f32[2,256]{1,0:T(2,128)S(1)} %pad_maximum_fusion.6), channel_id=1, source_target_pairs={{0,16},{16,32},{32,48},{48,64},{64,80},{80,96},{96,112},{112,128},... | collective-permute-start | bytes 6152 | tf_op jit(solution)/shard_map/ppermute | solution.py:22
  173.3 1.0 copy-start.4
  173.3 1.0 copy-start.6
  173.3 1.1 copy-start.10
  173.3 1.2 copy-start.12
  173.3 1.2 copy-start.14
  173.3 1.3 copy-start.16
  173.3 1.4 copy-start.18
  173.3 1.5 copy-start.20
  174.8 0.9 copy-start.8
  174.8 1.0 copy-start.21

commit v2 on v1

--- a/solution.py
+++ b/solution.py
@@ -16,16 +16,11 @@
 MESH = pl.DeviceIdType.MESH
 
 
-def from_behind(value, axis, steps):
-    count = lax.axis_size(axis)
-    first, last = (max(0, -steps), min(count, count - steps))
-    return lax.ppermute(value, axis, [(source, source + steps) for source in range(first, last)])
-
-
 def exchange_kernel(
-    meta_ref, obs_ref, out_ref, wsum_ref,
+    meta_ref, ice_ref, vel_ref, visc_ref, fric_ref, drive_ref, obs_ref, out_ref,
+    relax, first, second, q_one, q_two, misfit, lift, edge, halo,
     meta, ag, table, part, part_w, rp1, rp, rm1, rm, rw,
-    own_sem, meta_s, meta_r, ag_s, ag_r, rs_s, rs_r, rw_s, rw_r,
+    own_sem, meta_s, meta_r, ag_s, ag_r, rs_s, rs_r, rw_s, rw_r, edge_s, edge_r,
 ):
     chunks = ag.shape[1]
     scenes = ag.shape[2]
@@ -38,6 +33,20 @@
     z_right = (lax.rem(z + 1, NZ) * NX + x, me_y)
     z_left = (lax.rem(z + NZ - 1, NZ) * NX + x, me_y)
 
+    gx_next, gx_back = lax.rem(me_x + 1, NX * NZ), lax.rem(me_x + NX * NZ - 1, NX * NZ)
+    side_y = lax.axis_size("gy")
+    gy_next, gy_back = lax.rem(me_y + 1, side_y), lax.rem(me_y + side_y - 1, side_y)
+    at_first_x, at_last_x = me_x == 0, me_x == NX * NZ - 1
+    at_first_y, at_last_y = me_y == 0, me_y == side_y - 1
+    edges = (
+        (0, (gx_back, me_y)),
+        (1, (gx_next, me_y)),
+        (2, (me_x, gy_back)),
+        (3, (me_x, gy_next)),
+        (1, (gx_next, gy_back)),
+        (0, (gx_back, gy_next)),
+    )
+
     def remote(src, dst, send, recv, device):
         return pltpu.make_async_remote_copy(
             src_ref=src, dst_ref=dst, send_sem=send, recv_sem=recv, device_id=device, device_id_type=MESH
@@ -84,18 +93,130 @@
             part_w.at[source], rw.at[index], rw_s.at[index], rw_r.at[index], (z_right, z_left)[side]
         )
 
+    def edge_send(e, place):
+        message, device = edges[place]
+        return remote(
+            edge.at[e, message], halo.at[e, place], edge_s.at[e, place], edge_r.at[e, place], device
+        )
+
     barrier = pltpu.get_barrier_semaphore()
-    for device in (x_right, x_left, x_far, z_right, z_left):
+    for device in (x_right, x_left, x_far, z_right, z_left, *(device for _, device in edges)):
         pl.semaphore_signal(barrier, inc=1, device_id=device, device_id_type=MESH)
     for c in range(chunks):
         own_load(c).start()
-    pl.semaphore_wait(barrier, 5)
+    pl.semaphore_wait(barrier, 11)
 
     for peer in range(3):
         meta_send(peer).start()
     for c in range(LEAD):
         own_send(0, c).start()
         own_send(1, c).start()
+
+    cells = visc_ref.shape[0]
+    row_of = lax.broadcasted_iota(jnp.int32, (cells, 1), 0)
+    lane_of = lax.broadcasted_iota(jnp.int32, (1, cells), 1)
+
+    def send_edges(e, u, v, visc=None):
+        edge[e, 0, 0:1, :] = u[0:1, :]
+        edge[e, 0, 1:2, :] = v[0:1, :]
+        edge[e, 1, 0:1, :] = u[cells - 1 :, :]
+        edge[e, 1, 1:2, :] = v[cells - 1 :, :]
+        lane = lane_of[:, :128]
+        packed = jnp.where(lane == 0, u[:, :128], pltpu.roll(v[:, :128], 1, 1))
+        packed = jnp.where(lane == 2, pltpu.roll(u[:, cells - 128 :], 3, 1), packed)
+        packed = jnp.where(lane == 3, pltpu.roll(v[:, cells - 128 :], 4, 1), packed)
+        if visc is not None:
+            edge[e, 1, 2:3, :] = visc[cells - 1 :, :]
+            packed = jnp.where(lane == 4, pltpu.roll(visc[:, cells - 128 :], 5, 1), packed)
+        turned = packed.T
+        edge[e, 2, 0:2, :] = turned[0:2]
+        edge[e, 3, 0:3, :] = turned[2:5]
+        for place in range(6):
+            edge_send(e, place).start()
+
+    def lower_x(field, row):
+        return jnp.where(row_of == 0, row, pltpu.roll(field, 1, 0))
+
+    def lower_y(field, column):
+        return jnp.where(lane_of == 0, column, pltpu.roll(field, 1, 1))
+
+    def stress_image(e, u, v, visc):
+        for place in range(6):
+            edge_send(e, place).wait_recv()
+
+        def got(place, r):
+            return halo[e, place, r : r + 1, :]
+
+        zero = jnp.zeros((1, cells), jnp.float32)
+        up_x = [jnp.where(at_last_x, zero, got(0, r)) for r in range(2)]
+        up_y = [jnp.where(at_last_y, zero, got(2, r)) for r in range(2)]
+        visc_x = jnp.where(at_first_x, zero, halo[0, 1, 2:3, :])
+        visc_y = jnp.where(at_first_y, zero, halo[0, 3, 2:3, :])
+        back_x = [got(1, r) for r in range(2)]
+        back_y = [got(3, r) for r in range(2)]
+        back_x_up, back_y_up = [], []
+        for r in range(2):
+            corner = jnp.where(at_last_y, 0.0, halo[e, 4, r : r + 1, 0:1])
+            back_x_up.append(jnp.where(lane_of == cells - 1, corner, pltpu.roll(back_x[r], cells - 1, 1)))
+            corner = jnp.where(at_last_x, 0.0, halo[e, 5, r : r + 1, cells - 1 : cells])
+            back_y_up.append(jnp.where(lane_of == cells - 1, corner, pltpu.roll(back_y[r], cells - 1, 1)))
+        sxx_x = visc_x * (4.0 * (u[0:1, :] - back_x[0]) + 2.0 * (back_x_up[1] - back_x[1]))
+        sxy_x = visc_x * ((back_x_up[0] - back_x[0]) + (v[0:1, :] - back_x[1]))
+        u_y, v_y = edge[e, 2, 0:1, :], edge[e, 2, 1:2, :]
+        sxy_y = visc_y * ((u_y - back_y[0]) + (back_y_up[1] - back_y[1]))
+        syy_y = visc_y * (4.0 * (v_y - back_y[1]) + 2.0 * (back_y_up[0] - back_y[0]))
+        columns = jnp.concatenate([up_y[0], up_y[1], sxy_y, syy_y, visc_y, zero, zero, zero], axis=0).T
+        column = [columns[:, r : r + 1] for r in range(5)]
+        a_x = jnp.where(row_of == cells - 1, up_x[0], pltpu.roll(u, cells - 1, 0)) - u
+        b_x = jnp.where(row_of == cells - 1, up_x[1], pltpu.roll(v, cells - 1, 0)) - v
+        a_y = jnp.where(lane_of == cells - 1, column[0], pltpu.roll(u, cells - 1, 1)) - u
+        b_y = jnp.where(lane_of == cells - 1, column[1], pltpu.roll(v, cells - 1, 1)) - v
+        sxx = visc * (4.0 * a_x + 2.0 * b_y)
+        syy = visc * (4.0 * b_y + 2.0 * a_x)
+        sxy = visc * (a_y + b_x)
+        push_u = lower_x(sxx, sxx_x) - sxx + lower_y(sxy, column[2]) - sxy
+        push_v = lower_x(sxy, sxy_x) - sxy + lower_y(syy, column[3]) - syy
+        return (push_u, push_v), visc_x, column[4]
+
+    def first_sweep():
+        visc, fric = visc_ref[...], fric_ref[...]
+        start = [vel_ref[r].astype(jnp.float32) for r in range(2)]
+        push, row, column = stress_image(0, start[0], start[1], visc)
+        visc_x, visc_y = lower_x(visc, row), lower_y(visc, column)
+        diag = (5.0 * visc + 4.0 * visc_x + visc_y, 5.0 * visc + visc_x + 4.0 * visc_y)
+        for r in range(2):
+            relax_r = 1.0 / (diag[r] + fric)
+            relax[r] = relax_r
+            moved = relax_r * (drive_ref[r].astype(jnp.float32) - push[r] - fric * start[r])
+            q_one[r] = moved + start[r]
+            first[r] = start[r] + OMEGA * moved
+        send_edges(1, first[0], first[1])
+
+    def second_sweep():
+        fric = fric_ref[...]
+        push, _, _ = stress_image(1, first[0], first[1], visc_ref[...])
+        for r in range(2):
+            moved = relax[r] * (drive_ref[r].astype(jnp.float32) - push[r] - fric * first[r])
+            q_two[r] = moved + first[r]
+            second[r] = first[r] + OMEGA * moved
+
+    def adjoint():
+        fric = fric_ref[...]
+        u, v = lift[0], lift[1]
+        send_edges(2, u, v)
+        push, _, _ = stress_image(2, u, v, visc_ref[...])
+        total = None
+        for r in range(2):
+            lift_one = OMEGA * relax[r] * (misfit[r] - push[r] - fric * lift[r])
+            term = lift_one * q_one[r] + lift[r] * q_two[r]
+            total = term if total is None else total + term
+        tile = cells // 2
+        for s in range(SLOTS):
+            i, j = s // 2 * tile, s % 2 * tile
+            out_ref[i : i + tile, j : j + tile] = -ice(s) * total[i : i + tile, j : j + tile]
+
+    def ice(s):
+        return ice_ref[s // 2, s % 2].astype(jnp.float32)
 
     width = scenes * ROWS
     count = NZ * SLOTS * ROWS
@@ -129,6 +250,7 @@
     ring_send_w(1, 1).start()
     for c in range(chunks):
         own_load(c).wait()
+    send_edges(0, vel_ref[0].astype(jnp.float32), vel_ref[1].astype(jnp.float32), visc_ref[...])
 
     def at_chunk(c, action):
         pl.when(jnp.logical_and(c >= 0, c < chunks))(lambda: action(c))
@@ -162,7 +284,19 @@
     def finish(c):
         for side in range(2):
             ring_send(side, 4, c).wait_recv()
-        out_ref[:, rows(c), :] = part[c, 0] + (rp[2, c] + rm[2, c])
+        obs_sum = part[c, 0] + (rp[2, c] + rm[2, c])
+        tile = cells // 2
+        component = c // (chunks // 2)
+        offset = lax.rem(c, chunks // 2) * ROWS
+        for s in range(SLOTS):
+            at = (
+                component,
+                pl.ds(pl.multiple_of(s // 2 * tile + offset, ROWS), ROWS),
+                slice(s % 2 * tile, s % 2 * tile + tile),
+            )
+            value = ice(s) * (part_w[0, s : s + 1, :] * second[at] - obs_sum[s])
+            misfit[at] = value
+            lift[at] = OMEGA * relax[at] * value
 
     def ring_step_w(stage):
         for side in range(2):
@@ -170,6 +304,11 @@
             mine = 5 - stage if side == 0 else 3 + stage
             part_w[mine] += rw[side * 4 + stage - 2]
             ring_send_w(side, stage).start()
+
+    def finish_w():
+        for side in range(2):
+            ring_send_w(side, 4).wait_recv()
+        part_w[0] += rw[3] + rw[7]
 
     def step(k, carry):
         @pl.when(k + LEAD < chunks)
@@ -183,17 +322,18 @@
                 own_send(side, k).wait_recv()
                 far_send(side, k).start()
 
+        pl.when(k == 1 + 4 * GAP)(finish_w)
         at_chunk(k - 1 - 4 * GAP, finish)
         for stage in (4, 3, 2):
             at_chunk(k - 1 - (stage - 1) * GAP, functools.partial(ring_step, stage))
-            pl.when(k == stage + 1)(functools.partial(ring_step_w, stage))
+            pl.when(k == stage - 1)(functools.partial(ring_step_w, stage))
         at_chunk(k - 1, combine)
+        pl.when(k == 1)(first_sweep)
+        pl.when(k == 3)(second_sweep)
         return carry
 
     lax.fori_loop(0, chunks + 1 + 4 * GAP, step, 0)
-    for side in range(2):
-        ring_send_w(side, 4).wait_recv()
-    wsum_ref[...] = part_w[0] + (rw[3] + rw[7])
+    adjoint()
 
     def drain(c, carry):
         for side in range(2):
@@ -209,9 +349,14 @@
     for side in range(2):
         for stage in range(1, 5):
             ring_send_w(side, stage).wait_send()
-
-
-def exchange(obs, owners, slots, weights):
+    for e in range(3):
+        for place in range(6):
+            edge_send(e, place).wait_send()
+
+
+def body(vel0, visc, fric, drive, scene_obs, scene_weight, scene_owner, scene_slot, ice_mask):
+    obs, owners, slots, weights = scene_obs[0], scene_owner[0, :, 0], scene_slot[0], scene_weight[0]
+    cells = visc.shape[0]
     scenes, _, tile, _ = obs.shape
     height = 2 * tile
     chunks = height // ROWS
@@ -222,13 +367,18 @@
     dma = pltpu.SemaphoreType.DMA
     return pl.pallas_call(
         exchange_kernel,
-        out_shape=(
-            jax.ShapeDtypeStruct((SLOTS, height, tile), f32),
-            jax.ShapeDtypeStruct((8, 128), f32),
-        ),
-        in_specs=[pl.BlockSpec(memory_space=pltpu.VMEM), pl.BlockSpec(memory_space=pl.ANY)],
-        out_specs=(pl.BlockSpec(memory_space=pltpu.VMEM), pl.BlockSpec(memory_space=pltpu.VMEM)),
+        out_shape=jax.ShapeDtypeStruct((cells, cells), f32),
+        in_specs=[
+            pl.BlockSpec(memory_space=pltpu.VMEM),
+            pl.BlockSpec(memory_space=pltpu.SMEM),
+            *[pl.BlockSpec(memory_space=pltpu.VMEM)] * 4,
+            pl.BlockSpec(memory_space=pl.ANY),
+        ],
+        out_specs=pl.BlockSpec(memory_space=pltpu.VMEM),
         scratch_shapes=[
+            *[pltpu.VMEM((2, cells, cells), f32)] * 7,
+            pltpu.VMEM((3, 4, 8, cells), f32),
+            pltpu.VMEM((3, 6, 8, cells), f32),
             pltpu.VMEM((3, 8, scenes * ROWS), f32),
             pltpu.VMEM((4, chunks, scenes, ROWS, tile), bf16),
             pltpu.VMEM((NZ * SLOTS * ROWS, 4 * scenes * ROWS), bf16),
@@ -244,75 +394,12 @@
             dma((4, chunks)), dma((4, chunks)),
             dma((8, chunks)), dma((8, chunks)),
             dma((8,)), dma((8,)),
+            dma((3, 6)), dma((3, 6)),
         ],
         compiler_params=pltpu.CompilerParams(
             collective_id=0, has_side_effects=True, vmem_limit_bytes=48 * 1024 * 1024
         ),
-    )(meta, obs.reshape(scenes, height, tile))
-
-
-def stress_image(field, visc):
-    above_x = from_behind(field[:, :1, :], "gx", -1)
-    above_y = from_behind(field[:, :, :1], "gy", -1)
-    along_x = jnp.concatenate([field[:, 1:, :], above_x], axis=1) - field
-    along_y = jnp.concatenate([field[:, :, 1:], above_y], axis=2) - field
-    sxx = visc * (4.0 * along_x[0] + 2.0 * along_y[1])
-    syy = visc * (4.0 * along_y[1] + 2.0 * along_x[0])
-    sxy = visc * (along_y[0] + along_x[1])
-    below_x = from_behind(jnp.stack([sxx[-1], sxy[-1]]), "gx", 1)
-    below_y = from_behind(jnp.stack([sxy[:, -1], syy[:, -1]]), "gy", 1)
-    push_u = (
-        jnp.concatenate([below_x[0:1], sxx[:-1]], axis=0)
-        - sxx
-        + jnp.concatenate([below_y[0][:, None], sxy[:, :-1]], axis=1)
-        - sxy
-    )
-    push_v = (
-        jnp.concatenate([below_x[1:2], sxy[:-1]], axis=0)
-        - sxy
-        + jnp.concatenate([below_y[1][:, None], syy[:, :-1]], axis=1)
-        - syy
-    )
-    return jnp.stack([push_u, push_v])
-
-
-def spread_tiles(values, tiles_x, tiles_y, tile):
-    wide = jnp.broadcast_to(values.reshape(tiles_x, 1, tiles_y, 1), (tiles_x, tile, tiles_y, tile))
-    return wide.reshape(tiles_x * tile, tiles_y * tile)
-
-
-def body(vel0, visc, fric, drive, scene_obs, scene_weight, scene_owner, scene_slot, ice_mask):
-    cells_x, cells_y = visc.shape
-    tile = scene_obs.shape[-1]
-    tiles_x = cells_x // tile
-    tiles_y = cells_y // tile
-    summed, tile_weight = exchange(scene_obs[0], scene_owner[0, :, 0], scene_slot[0], scene_weight[0])
-    visc_row = from_behind(visc[-1:, :], "gx", 1)
-    visc_col = from_behind(visc[:, -1:], "gy", 1)
-    visc_x = jnp.concatenate([visc_row, visc[:-1]], axis=0)
-    visc_y = jnp.concatenate([visc_col, visc[:, :-1]], axis=1)
-    diag = jnp.stack([5.0 * visc + 4.0 * visc_x + visc_y, 5.0 * visc + visc_x + 4.0 * visc_y])
-    relax = 1.0 / (diag + fric)
-    start = vel0.astype(jnp.float32)
-    force = drive.astype(jnp.float32)
-    first_res = force - stress_image(start, visc) - fric * start
-    first = start + OMEGA * relax * first_res
-    second_res = force - stress_image(first, visc) - fric * first
-    second = first + OMEGA * relax * second_res
-    obs_sum = (
-        summed.reshape(tiles_x, tiles_y, 2, tile, tile)
-        .transpose(2, 0, 3, 1, 4)
-        .reshape(2, cells_x, cells_y)
-    )
-    weight_cell = spread_tiles(tile_weight[:SLOTS, 0], tiles_x, tiles_y, tile)
-    ice = spread_tiles(ice_mask.astype(jnp.float32), tiles_x, tiles_y, tile)
-    misfit_grad = ice * (weight_cell * second - obs_sum)
-    lift_two = OMEGA * relax * misfit_grad
-    back = misfit_grad - stress_image(lift_two, visc) - fric * lift_two
-    lift_one = OMEGA * relax * back
-    part_one = jnp.sum(lift_one * (relax * first_res + start), axis=0)
-    part_two = jnp.sum(lift_two * (relax * second_res + first), axis=0)
-    return -ice * (part_one + part_two)
+    )(meta, ice_mask, vel0, visc, fric, drive, obs.reshape(scenes, height, tile))
 
 
 def solution(mesh):

time: 177 us -> 115 us (0.65)
  the two profiles are of different devices: /device:TPU:88 before, /device:TPU:1 now
where the time goes in v2:
time: 115 us
  Pallas kernels  107 us (93%)
  local copies, waits for them, and re-layouts  8.04 us (7%)
    pallas_call x1, Pallas kernels, body(): pl.pallas_call(exchange_kernel, out_shape=jax.ShapeDtypeStruct((cells, ce...  107 us
    unnamed x19, local copies, waits for them, and re-layouts  7.66 us

profile of v2, /device:TPU:1, one launch (start us, length us, event | category | flops | bytes accessed | tf_op | source)
XLA Modules:
  0.0 114.7 jit_solution(8370296308150819636)
XLA Ops:
  0.0 0.0 copy-start.6
  0.0 0.7 copy-done.6
  0.7 0.0 copy-start.7
  0.7 0.0 copy-start.8
  0.7 0.6 copy-done.7
  1.3 0.0 copy-done.8
  1.3 0.1 pad.2.clone
  1.4 0.1 broadcast_in_dim.9
  1.5 0.1 broadcast_in_dim_reshape.6
  1.6 0.1 broadcast_in_dim.10
  1.6 0.1 broadcast_in_dim_reshape.7
  1.7 0.0 copy-start.5
  1.7 0.1 maximum_maximum_fusion.meta_ref
  1.8 0.6 copy-done.5
  2.4 0.0 copy-start
  2.4 1.2 %copy-done = bf16[1,16,2,128,128]{4,3,2,1,0:T(8,128)(2,1)S(1)} copy-done((bf16[1,16,2,128,128]{4,3,2,1,0:T(8,128)(2,1)S(1)}, bf16[1,16,2,128,128]{4,3,2,1,0:T(8,128)(2,1)}, u32[]{:S(2)}) %copy-start) | copy-done | bytes 1048600
  3.6 0.0 copy-start.1
  3.6 0.9 copy-done.1
  4.6 0.0 copy-start.2
  4.6 0.9 copy-done.2
  5.5 0.0 copy-start.3
  5.5 0.9 copy-done.3
  6.5 0.0 copy-start.4
  6.5 0.9 copy-done.4
  7.4 106.6 %shard_map.91 = f32[256,256]{1,0:T(8,128)S(1)} custom-call(f32[8,256]{1,0:T(8,128)S(1)} %maximum_maximum_fusion.meta_ref, s32[2,2]{1,0:T(2,128)S(1)} %copy-done.5, bf16[2,256,256]{2,1,0:T(8,128)(2,1)S(1)} %copy-done.1, f32[256,256]{1,0:T(8,128)S(1)} %copy-done.2, f32[256,256]{1,0:T(8,128)S(1)} %copy-done.3, bf16[2,256,256]{2,1,0:T(8,128)(2,1)S(1)} %copy-done.4, ...), custom_call_target="tpu_custom_call" | custom-call | tf_op jit(solution)/shard_map/pallas_call | solution.py:368
  114.0 0.7 copy.11
  (3 shorter events, 0.0 us)
Async XLA Ops:
  0.0 0.7 copy-start.6
  0.7 0.7 copy-start.7
  0.7 0.7 copy-start.8
  1.7 0.7 copy-start.5
  2.4 1.2 %copy-start = (bf16[1,16,2,128,128]{4,3,2,1,0:T(8,128)(2,1)S(1)}, bf16[1,16,2,128,128]{4,3,2,1,0:T(8,128)(2,1)}, u32[]{:S(2)}) copy-start(bf16[1,16,2,128,128]{4,3,2,1,0:T(8,128)(2,1)} %param.13) | copy-start | bytes 3145732
  3.6 0.9 copy-start.1
  4.6 0.9 copy-start.2
  5.5 0.9 copy-start.3
  6.5 0.9 copy-start.4

commit v3 on v2

--- a/solution.py
+++ b/solution.py
@@ -11,16 +11,17 @@
 NX, NZ = 4, 8
 SLOTS = 4
 ROWS = 16
-LEAD = 2
-GAP = 1
+LEAD = 3
+GAP = 2
 MESH = pl.DeviceIdType.MESH
 
 
 def exchange_kernel(
-    meta_ref, ice_ref, vel_ref, visc_ref, fric_ref, drive_ref, obs_ref, out_ref,
+    owner_in, slot_in, weight_in, ice_in, vel_in, visc_in, fric_in, drive_in, obs_ref, out_ref,
+    owner_ref, slot_ref, weight_ref, ice_ref, vel_ref, visc_ref, fric_ref, drive_ref, meta_ref,
     relax, first, second, q_one, q_two, misfit, lift, edge, halo,
     meta, ag, table, part, part_w, rp1, rp, rm1, rm, rw,
-    own_sem, meta_s, meta_r, ag_s, ag_r, rs_s, rs_r, rw_s, rw_r, edge_s, edge_r,
+    own_sem, meta_s, meta_r, ag_s, ag_r, rs_s, rs_r, rw_s, rw_r, edge_s, edge_r, load_sem,
 ):
     chunks = ag.shape[1]
     scenes = ag.shape[2]
@@ -102,8 +103,25 @@
     barrier = pltpu.get_barrier_semaphore()
     for device in (x_right, x_left, x_far, z_right, z_left, *(device for _, device in edges)):
         pl.semaphore_signal(barrier, inc=1, device_id=device, device_id_type=MESH)
+    pairs = (
+        (owner_in, owner_ref), (slot_in, slot_ref), (weight_in, weight_ref), (vel_in, vel_ref),
+        (visc_in, visc_ref), (fric_in, fric_ref), (drive_in, drive_ref), (ice_in, ice_ref),
+    )
+    loads = [pltpu.make_async_copy(a, b, load_sem.at[n]) for n, (a, b) in enumerate(pairs)]
+    for load in loads:
+        load.start()
     for c in range(chunks):
         own_load(c).start()
+    for load in loads[:3]:
+        load.wait()
+    key = (owner_ref[...] * SLOTS + slot_ref[...]).astype(jnp.float32)
+    place = lax.broadcasted_iota(jnp.int32, (scenes, scenes), 0)
+    same = place == lax.broadcasted_iota(jnp.int32, (scenes, scenes), 1)
+    spread = lax.broadcasted_iota(jnp.int32, (scenes, scenes * ROWS), 1) // ROWS
+    spread = spread == lax.broadcasted_iota(jnp.int32, (scenes, scenes * ROWS), 0)
+    for r, value in enumerate((key, weight_ref[...].astype(jnp.float32))):
+        column = jnp.sum(jnp.where(same, value, 0.0), axis=1, keepdims=True)
+        meta_ref[r : r + 1, :] = jnp.sum(jnp.where(spread, column, 0.0), axis=0, keepdims=True)
     pl.semaphore_wait(barrier, 11)
 
     for peer in range(3):
@@ -250,6 +268,8 @@
     ring_send_w(1, 1).start()
     for c in range(chunks):
         own_load(c).wait()
+    for load in loads[3:]:
+        load.wait()
     send_edges(0, vel_ref[0].astype(jnp.float32), vel_ref[1].astype(jnp.float32), visc_ref[...])
 
     def at_chunk(c, action):
@@ -355,27 +375,30 @@
 
 
 def body(vel0, visc, fric, drive, scene_obs, scene_weight, scene_owner, scene_slot, ice_mask):
-    obs, owners, slots, weights = scene_obs[0], scene_owner[0, :, 0], scene_slot[0], scene_weight[0]
+    obs = scene_obs[0]
     cells = visc.shape[0]
     scenes, _, tile, _ = obs.shape
     height = 2 * tile
     chunks = height // ROWS
-    key = jnp.repeat((owners * SLOTS + slots).astype(jnp.float32), ROWS)
-    weight = jnp.repeat(weights.astype(jnp.float32), ROWS)
-    meta = jnp.concatenate([key[None], weight[None], jnp.zeros((6, scenes * ROWS), jnp.float32)], axis=0)
     f32, bf16 = jnp.float32, jnp.bfloat16
     dma = pltpu.SemaphoreType.DMA
     return pl.pallas_call(
         exchange_kernel,
         out_shape=jax.ShapeDtypeStruct((cells, cells), f32),
         in_specs=[
-            pl.BlockSpec(memory_space=pltpu.VMEM),
-            pl.BlockSpec(memory_space=pltpu.SMEM),
-            *[pl.BlockSpec(memory_space=pltpu.VMEM)] * 4,
-            pl.BlockSpec(memory_space=pl.ANY),
-        ],
+            pl.BlockSpec(memory_space=pltpu.HBM)
+        ] * 9,
         out_specs=pl.BlockSpec(memory_space=pltpu.VMEM),
         scratch_shapes=[
+            pltpu.VMEM((1, scenes), jnp.int32),
+            pltpu.VMEM((1, scenes), jnp.int32),
+            pltpu.VMEM((1, scenes), bf16),
+            pltpu.SMEM((2, 2), jnp.int32),
+            pltpu.VMEM((2, cells, cells), bf16),
+            pltpu.VMEM((cells, cells), f32),
+            pltpu.VMEM((cells, cells), f32),
+            pltpu.VMEM((2, cells, cells), bf16),
+            pltpu.VMEM((8, scenes * ROWS), f32),
             *[pltpu.VMEM((2, cells, cells), f32)] * 7,
             pltpu.VMEM((3, 4, 8, cells), f32),
             pltpu.VMEM((3, 6, 8, cells), f32),
@@ -395,11 +418,12 @@
             dma((8, chunks)), dma((8, chunks)),
             dma((8,)), dma((8,)),
             dma((3, 6)), dma((3, 6)),
+            dma((8,)),
         ],
         compiler_params=pltpu.CompilerParams(
-            collective_id=0, has_side_effects=True, vmem_limit_bytes=48 * 1024 * 1024
+            collective_id=0, has_side_effects=True, vmem_limit_bytes=67043328
         ),
-    )(meta, ice_mask, vel0, visc, fric, drive, obs.reshape(scenes, height, tile))
+    )(scene_owner.reshape(1, scenes), scene_slot, scene_weight, ice_mask, vel0, visc, fric, drive, obs.reshape(scenes, height, tile))
 
 
 def solution(mesh):

time: 115 us -> 92.4 us (0.80)
  Pallas kernels: 107 us -> 90.6 us
  local copies, waits for them, and re-layouts: 8.04 us -> 1.67 us
    pallas_call x1, Pallas kernels: 107 us -> 90.6 us  [body(): pl.pallas_call(exchange_kernel, out_shape=jax.ShapeDtypeStruct((cells, ce...]
    unnamed x19 -> x1, local copies, waits for them, and re-layouts: 7.66 us -> 1.67 us
where the time goes in v3:
time: 92.4 us; the launch traced here: 92.3 us
  Pallas kernels  90.6 us (98%)
  local copies, waits for them, and re-layouts  1.67 us (2%)
    pallas_call x1, Pallas kernels, body(): pl.pallas_call(exchange_kernel, out_shape=jax.ShapeDtypeStruct((cells, ce...  90.6 us

profile of v3, /device:TPU:1, one launch (start us, length us, event | category | flops | bytes accessed | tf_op | source)
XLA Modules:
  0.0 92.3 jit_solution(9335076255700326206)
XLA Ops:
  0.0 90.6 %shard_map.91 = f32[256,256]{1,0:T(8,128)} custom-call(s32[1,16]{1,0:T(1,128)} %bitcast.3, s32[1,16]{1,0:T(1,128)} %slot_in.1, bf16[1,16]{1,0:T(2,128)(2,1)} %weight_in.1, s32[2,2]{1,0:T(2,128)} %ice_in.1, bf16[2,256,256]{2,1,0:T(8,128)(2,1)} %vel_in.1, f32[256,256]{1,0:T(8,128)} %visc_in.1, f32[256,256]{1,0:T(8,128)} %fric_in.1, ...), custom_call_target="tpu_custom_call" | custom-call | tf_op jit(solution)/shard_map/pallas_call | solution.py:385
  90.6 1.7 %copy.11 = f32[256,256]{1,0:T(8,128)} copy(f32[256,256]{1,0:T(8,128)} %shard_map.91) | data formatting | bytes 524288

commit v4 on v3

--- a/solution.py
+++ b/solution.py
@@ -10,6 +10,7 @@
 OMEGA = 0.6
 NX, NZ = 4, 8
 SLOTS = 4
+STRIP = 32
 ROWS = 16
 LEAD = 3
 GAP = 2
@@ -19,7 +20,7 @@
 def exchange_kernel(
     owner_in, slot_in, weight_in, ice_in, vel_in, visc_in, fric_in, drive_in, obs_ref, out_ref,
     owner_ref, slot_ref, weight_ref, ice_ref, vel_ref, visc_ref, fric_ref, drive_ref, meta_ref,
-    relax, first, second, q_one, q_two, misfit, lift, edge, halo,
+    relax, first, second, gain, q_two, misfit, lift, edge, halo, gain_edge,
     meta, ag, table, part, part_w, rp1, rp, rm1, rm, rw,
     own_sem, meta_s, meta_r, ag_s, ag_r, rs_s, rs_r, rw_s, rw_r, edge_s, edge_r, load_sem,
 ):
@@ -131,34 +132,32 @@
         own_send(1, c).start()
 
     cells = visc_ref.shape[0]
-    row_of = lax.broadcasted_iota(jnp.int32, (cells, 1), 0)
     lane_of = lax.broadcasted_iota(jnp.int32, (1, cells), 1)
 
+    def columns_of(*columns):
+        lane, packed = lane_of[:, :128], None
+        for n, (last, array) in enumerate(columns):
+            block = array[:, cells - 128 :] if last else array[:, :128]
+            moved = (n + 1 if last else n) % 128
+            block = pltpu.roll(block, moved, 1) if moved else block
+            packed = block if packed is None else jnp.where(lane == n, block, packed)
+        return packed.T
+
     def send_edges(e, u, v, visc=None):
-        edge[e, 0, 0:1, :] = u[0:1, :]
-        edge[e, 0, 1:2, :] = v[0:1, :]
-        edge[e, 1, 0:1, :] = u[cells - 1 :, :]
-        edge[e, 1, 1:2, :] = v[cells - 1 :, :]
-        lane = lane_of[:, :128]
-        packed = jnp.where(lane == 0, u[:, :128], pltpu.roll(v[:, :128], 1, 1))
-        packed = jnp.where(lane == 2, pltpu.roll(u[:, cells - 128 :], 3, 1), packed)
-        packed = jnp.where(lane == 3, pltpu.roll(v[:, cells - 128 :], 4, 1), packed)
+        for r, array in enumerate((u, v)):
+            edge[e, 0, r : r + 1, :] = array[0:1, :]
+            edge[e, 1, r : r + 1, :] = array[cells - 1 :, :]
+        columns = [(False, u), (False, v), (True, u), (True, v)]
         if visc is not None:
             edge[e, 1, 2:3, :] = visc[cells - 1 :, :]
-            packed = jnp.where(lane == 4, pltpu.roll(visc[:, cells - 128 :], 5, 1), packed)
-        turned = packed.T
+            columns.append((True, visc))
+        turned = columns_of(*columns)
         edge[e, 2, 0:2, :] = turned[0:2]
         edge[e, 3, 0:3, :] = turned[2:5]
         for place in range(6):
             edge_send(e, place).start()
 
-    def lower_x(field, row):
-        return jnp.where(row_of == 0, row, pltpu.roll(field, 1, 0))
-
-    def lower_y(field, column):
-        return jnp.where(lane_of == 0, column, pltpu.roll(field, 1, 1))
-
-    def stress_image(e, u, v, visc):
+    def outside(e, u_first, v_first):
         for place in range(6):
             edge_send(e, place).wait_recv()
 
@@ -178,100 +177,174 @@
             back_x_up.append(jnp.where(lane_of == cells - 1, corner, pltpu.roll(back_x[r], cells - 1, 1)))
             corner = jnp.where(at_last_x, 0.0, halo[e, 5, r : r + 1, cells - 1 : cells])
             back_y_up.append(jnp.where(lane_of == cells - 1, corner, pltpu.roll(back_y[r], cells - 1, 1)))
-        sxx_x = visc_x * (4.0 * (u[0:1, :] - back_x[0]) + 2.0 * (back_x_up[1] - back_x[1]))
-        sxy_x = visc_x * ((back_x_up[0] - back_x[0]) + (v[0:1, :] - back_x[1]))
+        sxx_x = visc_x * (4.0 * (u_first - back_x[0]) + 2.0 * (back_x_up[1] - back_x[1]))
+        sxy_x = visc_x * ((back_x_up[0] - back_x[0]) + (v_first - back_x[1]))
         u_y, v_y = edge[e, 2, 0:1, :], edge[e, 2, 1:2, :]
         sxy_y = visc_y * ((u_y - back_y[0]) + (back_y_up[1] - back_y[1]))
         syy_y = visc_y * (4.0 * (v_y - back_y[1]) + 2.0 * (back_y_up[0] - back_y[0]))
-        columns = jnp.concatenate([up_y[0], up_y[1], sxy_y, syy_y, visc_y, zero, zero, zero], axis=0).T
-        column = [columns[:, r : r + 1] for r in range(5)]
-        a_x = jnp.where(row_of == cells - 1, up_x[0], pltpu.roll(u, cells - 1, 0)) - u
-        b_x = jnp.where(row_of == cells - 1, up_x[1], pltpu.roll(v, cells - 1, 0)) - v
-        a_y = jnp.where(lane_of == cells - 1, column[0], pltpu.roll(u, cells - 1, 1)) - u
-        b_y = jnp.where(lane_of == cells - 1, column[1], pltpu.roll(v, cells - 1, 1)) - v
-        sxx = visc * (4.0 * a_x + 2.0 * b_y)
-        syy = visc * (4.0 * b_y + 2.0 * a_x)
-        sxy = visc * (a_y + b_x)
-        push_u = lower_x(sxx, sxx_x) - sxx + lower_y(sxy, column[2]) - sxy
-        push_v = lower_x(sxy, sxy_x) - sxy + lower_y(syy, column[3]) - syy
-        return (push_u, push_v), visc_x, column[4]
+        return up_x, up_y, visc_x, visc_y, sxx_x, sxy_x, sxy_y, syy_y
+
+    def as_columns(*rows):
+        zero = jnp.zeros((8 - len(rows), cells), jnp.float32)
+        turned = jnp.concatenate([*rows, zero], axis=0).T
+        return [turned[:, n : n + 1] for n in range(len(rows))]
+
+    strip_row = lax.broadcasted_iota(jnp.int32, (STRIP, 1), 0)
+
+    def upper_x(field, row):
+        return jnp.where(strip_row == STRIP - 1, row, pltpu.roll(field, STRIP - 1, 0))
+
+    def lower_x(field, row):
+        return jnp.where(strip_row == 0, row, pltpu.roll(field, 1, 0))
+
+    def upper_y(field, column):
+        return jnp.where(lane_of == cells - 1, column, pltpu.roll(field, cells - 1, 1))
+
+    def lower_y(field, column):
+        return jnp.where(lane_of == 0, column, pltpu.roll(field, 1, 1))
+
+    def stress_images(field, up_x, up_y, sxx_x, sxy_x, sxy_y, syy_y, apply):
+        for i in range(0, cells, STRIP):
+            rows_i = slice(i, i + STRIP)
+            u, v = field(0, rows_i), field(1, rows_i)
+            following = slice(i + STRIP, i + STRIP + 1)
+            after = up_x if i + STRIP == cells else [field(r, following) for r in range(2)]
+            a_x, b_x = upper_x(u, after[0]) - u, upper_x(v, after[1]) - v
+            a_y = upper_y(u, take(up_y[0], rows_i)) - u
+            b_y = upper_y(v, take(up_y[1], rows_i)) - v
+            visc = visc_ref[rows_i, :]
+            sxx = visc * (4.0 * a_x + 2.0 * b_y)
+            syy = visc * (4.0 * b_y + 2.0 * a_x)
+            sxy = visc * (a_y + b_x)
+            push_u = lower_x(sxx, sxx_x) - sxx + lower_y(sxy, take(sxy_y, rows_i)) - sxy
+            push_v = lower_x(sxy, sxy_x) - sxy + lower_y(syy, take(syy_y, rows_i)) - syy
+            apply(rows_i, (u, v), (push_u, push_v))
+            sxx_x, sxy_x = sxx[STRIP - 1 :, :], sxy[STRIP - 1 :, :]
+
+    def take(column, rows_i):
+        return column if isinstance(column, float) else column[rows_i, :]
+
+    def ice_row(rows_i):
+        s = rows_i.start // (cells // 2) * 2
+        return jnp.where(lane_of < cells // 2, ice(s), ice(s + 1))
 
     def first_sweep():
-        visc, fric = visc_ref[...], fric_ref[...]
-        start = [vel_ref[r].astype(jnp.float32) for r in range(2)]
-        push, row, column = stress_image(0, start[0], start[1], visc)
-        visc_x, visc_y = lower_x(visc, row), lower_y(visc, column)
-        diag = (5.0 * visc + 4.0 * visc_x + visc_y, 5.0 * visc + visc_x + 4.0 * visc_y)
-        for r in range(2):
-            relax_r = 1.0 / (diag[r] + fric)
-            relax[r] = relax_r
-            moved = relax_r * (drive_ref[r].astype(jnp.float32) - push[r] - fric * start[r])
-            q_one[r] = moved + start[r]
-            first[r] = start[r] + OMEGA * moved
-        send_edges(1, first[0], first[1])
+        def field(r, rows_i):
+            return vel_ref[r, rows_i, :].astype(jnp.float32)
+
+        up_x, up_y, visc_x, visc_y, sxx_x, sxy_x, sxy_y, syy_y = outside(0, field(0, slice(0, 1)), field(1, slice(0, 1)))
+        *columns, visc_y = as_columns(up_y[0], up_y[1], sxy_y, syy_y, visc_y)
+
+        def apply(rows_i, start, push):
+            visc, fric = visc_ref[rows_i, :], fric_ref[rows_i, :]
+            before = visc_x if rows_i.start == 0 else visc_ref[rows_i.start - 1 : rows_i.start, :]
+            behind_x, behind_y = lower_x(visc, before), lower_y(visc, visc_y[rows_i, :])
+            diag = (5.0 * visc + 4.0 * behind_x + behind_y, 5.0 * visc + behind_x + 4.0 * behind_y)
+            for r in range(2):
+                relax_r = 1.0 / (diag[r] + fric)
+                relax[r, rows_i, :] = OMEGA * relax_r
+                moved = relax_r * (drive_ref[r, rows_i, :].astype(jnp.float32) - push[r] - fric * start[r])
+                gain[r, rows_i, :] = ice_row(rows_i) * (OMEGA * relax_r) * (moved + start[r])
+                first[r, rows_i, :] = start[r] + OMEGA * moved
+
+        stress_images(field, up_x, columns[:2], sxx_x, sxy_x, columns[2], columns[3], apply)
+        send_edges(1, first.at[0], first.at[1])
 
     def second_sweep():
-        fric = fric_ref[...]
-        push, _, _ = stress_image(1, first[0], first[1], visc_ref[...])
-        for r in range(2):
-            moved = relax[r] * (drive_ref[r].astype(jnp.float32) - push[r] - fric * first[r])
-            q_two[r] = moved + first[r]
-            second[r] = first[r] + OMEGA * moved
+        def field(r, rows_i):
+            return first[r, rows_i, :]
+
+        up_x, up_y, _, _, sxx_x, sxy_x, sxy_y, syy_y = outside(1, field(0, slice(0, 1)), field(1, slice(0, 1)))
+        columns = as_columns(up_y[0], up_y[1], sxy_y, syy_y)
+
+        def apply(rows_i, start, push):
+            fric = fric_ref[rows_i, :]
+            for r in range(2):
+                residual = drive_ref[r, rows_i, :].astype(jnp.float32) - push[r] - fric * start[r]
+                moved = relax[r, rows_i, :] * residual
+                q_two[r, rows_i, :] = ice_row(rows_i) * ((1.0 / OMEGA) * moved + start[r])
+                second[r, rows_i, :] = start[r] + moved
+
+        stress_images(field, up_x, columns[:2], sxx_x, sxy_x, columns[2], columns[3], apply)
+        gains = columns_of((False, gain.at[0]), (False, gain.at[1]), (True, gain.at[0]), (True, gain.at[1]))
+        gain_edge[0:4, :] = gains[0:4]
 
     def adjoint():
-        fric = fric_ref[...]
-        u, v = lift[0], lift[1]
-        send_edges(2, u, v)
-        push, _, _ = stress_image(2, u, v, visc_ref[...])
-        total = None
-        for r in range(2):
-            lift_one = OMEGA * relax[r] * (misfit[r] - push[r] - fric * lift[r])
-            term = lift_one * q_one[r] + lift[r] * q_two[r]
-            total = term if total is None else total + term
-        tile = cells // 2
-        for s in range(SLOTS):
-            i, j = s // 2 * tile, s % 2 * tile
-            out_ref[i : i + tile, j : j + tile] = -ice(s) * total[i : i + tile, j : j + tile]
+        def field(r, rows_i):
+            return lift[r, rows_i, :]
+
+        send_edges(2, lift.at[0], lift.at[1])
+
+        def apply(rows_i, lifted, push):
+            fric = fric_ref[rows_i, :]
+            total = None
+            for r in range(2):
+                back = push[r] - misfit[r, rows_i, :] + fric * lifted[r]
+                term = gain[r, rows_i, :] * back - q_two[r, rows_i, :] * lifted[r]
+                total = term if total is None else total + term
+            out_ref[rows_i, :] = total
+
+        zero = jnp.zeros((1, cells), jnp.float32)
+        stress_images(field, (zero, zero), (0.0, 0.0), zero, zero, 0.0, 0.0, apply)
+        up_x, up_y, _, _, sxx_x, sxy_x, sxy_y, syy_y = outside(2, field(0, slice(0, 1)), field(1, slice(0, 1)))
+        end = slice(cells - 1, cells)
+        visc = visc_ref[end, :]
+        sxx, syy, sxy = 4.0 * visc * up_x[0], 2.0 * visc * up_x[0], visc * up_x[1]
+        push_u = lower_y(sxy, 0.0) - sxy - sxx
+        push_v = lower_y(syy, 0.0) - syy - sxy
+        out_ref[0:1, :] += gain[0, 0:1, :] * sxx_x + gain[1, 0:1, :] * sxy_x
+        out_ref[end, :] += gain[0, end, :] * push_u + gain[1, end, :] * push_v
+        visc = edge[0, 3, 2:3, :]
+        sxx, syy, sxy = 2.0 * visc * up_y[1], 4.0 * visc * up_y[1], visc * up_y[0]
+        push_u = lower_y(sxx, 0.0) - sxx - sxy
+        push_v = lower_y(sxy, 0.0) - sxy - syy
+        column_first, column_last = as_columns(
+            gain_edge[0:1, :] * sxy_y + gain_edge[1:2, :] * syy_y,
+            gain_edge[2:3, :] * push_u + gain_edge[3:4, :] * push_v,
+        )
+        lane = lane_of[:, :128]
+        out_ref[:, :128] += jnp.where(lane == 0, column_first, 0.0)
+        out_ref[:, cells - 128 :] += jnp.where(lane == 127, column_last, 0.0)
 
     def ice(s):
         return ice_ref[s // 2, s % 2].astype(jnp.float32)
 
     width = scenes * ROWS
-    count = NZ * SLOTS * ROWS
+    diagonal = lax.broadcasted_iota(jnp.int32, (ROWS, width), 0) == lax.bitwise_and(
+        lax.broadcasted_iota(jnp.int32, (ROWS, width), 1), ROWS - 1
+    )
 
     def fill(source, block):
         key, weight = block[0:1, :], block[1:2, :]
-        row = lax.broadcasted_iota(jnp.int32, (count, 1), 0)
-        lane = lax.broadcasted_iota(jnp.int32, (1, width), 1)
-        target_z = lax.rem(z + row // (SLOTS * ROWS), NZ)
-        want = (target_z * NX + x) * SLOTS + lax.rem(row // ROWS, SLOTS)
-        want = want.astype(jnp.float32)
-        hit = jnp.logical_and(key == want, lax.rem(lane, ROWS) == lax.rem(row, ROWS))
-        table[:, source * width : (source + 1) * width] = jnp.where(hit, weight, 0.0).astype(jnp.bfloat16)
-        row = lax.broadcasted_iota(jnp.int32, (NZ * 8, 1), 0)
-        slot = lax.rem(row, 8)
-        target_z = lax.rem(z + row // 8, NZ)
-        want = jnp.where(slot < SLOTS, (target_z * NX + x) * SLOTS + slot, -1).astype(jnp.float32)
-        hit = jnp.logical_and(key == want, lax.rem(lane, ROWS) == 0)
-        return jnp.sum(jnp.where(hit, weight, 0.0), axis=1, keepdims=True)
-
-    total_w = fill(0, meta_ref[...])
+        for distance in range(NZ):
+            owner = lax.rem(z + distance, NZ) * NX + x
+            for slot in range(SLOTS):
+                want = (owner * SLOTS + slot).astype(jnp.float32)
+                chosen = jnp.where(key == want, weight, 0.0)
+                at = (distance * SLOTS + slot) * ROWS
+                table[at : at + ROWS, source * width : (source + 1) * width] = jnp.where(
+                    diagonal, chosen, 0.0
+                ).astype(jnp.bfloat16)
+
+    for load in loads[3:]:
+        load.wait()
+    send_edges(0, vel_ref[0].astype(jnp.float32), vel_ref[1].astype(jnp.float32), visc_ref)
+    fill(0, meta_ref[...])
     for peer in range(3):
         meta_send(peer).wait_recv()
-        total_w = total_w + fill(1 + peer, meta[peer])
-    total_w = jnp.broadcast_to(total_w, (NZ * 8, 128)).reshape(NZ, 8, 128)
-    part_w[0:NZ] = total_w
-    slot = lax.broadcasted_iota(jnp.int32, (8, 128), 0)
-    part_w[4] = jnp.where(slot < 2, total_w[4], 0.0)
-    part_w[8] = jnp.where(slot < 2, 0.0, total_w[4])
+        fill(1 + peer, meta[peer])
+    ones = jnp.ones((4 * width, 128), jnp.bfloat16)
+    total_w = jnp.dot(table[...], ones, preferred_element_type=jnp.float32)
+    part_w[...] = jnp.zeros_like(part_w)
+    for distance in range(NZ):
+        for slot in range(SLOTS):
+            at = (distance * SLOTS + slot) * ROWS
+            place = NZ if distance == NZ // 2 and slot >= 2 else distance
+            part_w[place, slot : slot + 1, :] = total_w[at : at + 1, :]
     ring_send_w(0, 1).start()
     ring_send_w(1, 1).start()
     for c in range(chunks):
         own_load(c).wait()
-    for load in loads[3:]:
-        load.wait()
-    send_edges(0, vel_ref[0].astype(jnp.float32), vel_ref[1].astype(jnp.float32), visc_ref[...])
-
     def at_chunk(c, action):
         pl.when(jnp.logical_and(c >= 0, c < chunks))(lambda: action(c))
 
@@ -316,7 +389,7 @@
             )
             value = ice(s) * (part_w[0, s : s + 1, :] * second[at] - obs_sum[s])
             misfit[at] = value
-            lift[at] = OMEGA * relax[at] * value
+            lift[at] = relax[at] * value
 
     def ring_step_w(stage):
         for side in range(2):
@@ -346,10 +419,10 @@
         at_chunk(k - 1 - 4 * GAP, finish)
         for stage in (4, 3, 2):
             at_chunk(k - 1 - (stage - 1) * GAP, functools.partial(ring_step, stage))
-            pl.when(k == stage - 1)(functools.partial(ring_step_w, stage))
+            pl.when(k == 2 * stage - 3)(functools.partial(ring_step_w, stage))
         at_chunk(k - 1, combine)
-        pl.when(k == 1)(first_sweep)
-        pl.when(k == 3)(second_sweep)
+        pl.when(k == 0)(first_sweep)
+        pl.when(k == 2)(second_sweep)
         return carry
 
     lax.fori_loop(0, chunks + 1 + 4 * GAP, step, 0)
@@ -402,6 +475,7 @@
             *[pltpu.VMEM((2, cells, cells), f32)] * 7,
             pltpu.VMEM((3, 4, 8, cells), f32),
             pltpu.VMEM((3, 6, 8, cells), f32),
+            pltpu.VMEM((8, cells), f32),
             pltpu.VMEM((3, 8, scenes * ROWS), f32),
             pltpu.VMEM((4, chunks, scenes, ROWS, tile), bf16),
             pltpu.VMEM((NZ * SLOTS * ROWS, 4 * scenes * ROWS), bf16),

time: 92.4 us -> 92.6 us (level); the launches traced: 92.3 us -> 91 us
  Pallas kernels: 90.6 us -> 89.3 us
    pallas_call x1, Pallas kernels: 90.6 us -> 89.3 us  [body(): pl.pallas_call(exchange_kernel, out_shape=jax.ShapeDtypeStruct((cells, ce...]
where the time goes in v4:
time: 92.6 us; the launch traced here: 91 us
  Pallas kernels  89.3 us (96%)
  local copies, waits for them, and re-layouts  1.67 us (2%)
    pallas_call x1, Pallas kernels, body(): pl.pallas_call(exchange_kernel, out_shape=jax.ShapeDtypeStruct((cells, ce...  89.3 us

profile of v4, /device:TPU:1, one launch (start us, length us, event | category | flops | bytes accessed | tf_op | source)
XLA Modules:
  0.0 91.0 jit_solution(2928253375541741789)
XLA Ops:
  0.0 89.3 %shard_map.91 = f32[256,256]{1,0:T(8,128)} custom-call(s32[1,16]{1,0:T(1,128)} %bitcast.3, s32[1,16]{1,0:T(1,128)} %slot_in.1, bf16[1,16]{1,0:T(2,128)(2,1)} %weight_in.1, s32[2,2]{1,0:T(2,128)} %ice_in.1, bf16[2,256,256]{2,1,0:T(8,128)(2,1)} %vel_in.1, f32[256,256]{1,0:T(8,128)} %visc_in.1, f32[256,256]{1,0:T(8,128)} %fric_in.1, ...), custom_call_target="tpu_custom_call" | custom-call | tf_op jit(solution)/shard_map/pallas_call | solution.py:458
  89.3 1.7 %copy.11 = f32[256,256]{1,0:T(8,128)} copy(f32[256,256]{1,0:T(8,128)} %shard_map.91) | data formatting | bytes 524288

commit v5 on v4

--- a/solution.py
+++ b/solution.py
@@ -286,6 +286,7 @@
 
         zero = jnp.zeros((1, cells), jnp.float32)
         stress_images(field, (zero, zero), (0.0, 0.0), zero, zero, 0.0, 0.0, apply)
+        wait_sends()
         up_x, up_y, _, _, sxx_x, sxy_x, sxy_y, syy_y = outside(2, field(0, slice(0, 1)), field(1, slice(0, 1)))
         end = slice(cells - 1, cells)
         visc = visc_ref[end, :]
@@ -403,17 +404,33 @@
             ring_send_w(side, 4).wait_recv()
         part_w[0] += rw[3] + rw[7]
 
+    def wait_sends():
+        def drain(c, carry):
+            for side in range(2):
+                own_send(side, c).wait_send()
+                far_send(side, c).wait_send()
+                for stage in range(1, 5):
+                    ring_send(side, stage, c).wait_send()
+            return carry
+
+        lax.fori_loop(0, chunks, drain, 0)
+        for peer in range(3):
+            meta_send(peer).wait_send()
+        for side in range(2):
+            for stage in range(1, 5):
+                ring_send_w(side, stage).wait_send()
+
     def step(k, carry):
-        @pl.when(k + LEAD < chunks)
-        def _():
-            own_send(0, k + LEAD).start()
-            own_send(1, k + LEAD).start()
-
         @pl.when(k < chunks)
         def _():
             for side in range(2):
                 own_send(side, k).wait_recv()
                 far_send(side, k).start()
+
+        @pl.when(k + LEAD < chunks)
+        def _():
+            own_send(0, k + LEAD).start()
+            own_send(1, k + LEAD).start()
 
         pl.when(k == 1 + 4 * GAP)(finish_w)
         at_chunk(k - 1 - 4 * GAP, finish)
@@ -427,21 +444,6 @@
 
     lax.fori_loop(0, chunks + 1 + 4 * GAP, step, 0)
     adjoint()
-
-    def drain(c, carry):
-        for side in range(2):
-            own_send(side, c).wait_send()
-            far_send(side, c).wait_send()
-            for stage in range(1, 5):
-                ring_send(side, stage, c).wait_send()
-        return carry
-
-    lax.fori_loop(0, chunks, drain, 0)
-    for peer in range(3):
-        meta_send(peer).wait_send()
-    for side in range(2):
-        for stage in range(1, 5):
-            ring_send_w(side, stage).wait_send()
     for e in range(3):
         for place in range(6):
             edge_send(e, place).wait_send()

time: 92.6 us -> 87.3 us (0.943); the launches traced: 91 us -> 86.8 us
  Pallas kernels: 89.3 us -> 85.1 us
    pallas_call x1, Pallas kernels: 89.3 us -> 85.1 us  [body(): pl.pallas_call(exchange_kernel, out_shape=jax.ShapeDtypeStruct((cells, ce...]
where the time goes in v5:
time: 87.3 us; the launch traced here: 86.8 us
  Pallas kernels  85.1 us (97%)
  local copies, waits for them, and re-layouts  1.67 us (2%)
    pallas_call x1, Pallas kernels, body(): pl.pallas_call(exchange_kernel, out_shape=jax.ShapeDtypeStruct((cells, ce...  85.1 us

profile of v5, /device:TPU:1, one launch (start us, length us, event | category | flops | bytes accessed | tf_op | source)
XLA Modules:
  0.0 86.8 jit_solution(6029931559632925068)
XLA Ops:
  0.0 85.1 %shard_map.91 = f32[256,256]{1,0:T(8,128)} custom-call(s32[1,16]{1,0:T(1,128)} %bitcast.3, s32[1,16]{1,0:T(1,128)} %slot_in.1, bf16[1,16]{1,0:T(2,128)(2,1)} %weight_in.1, s32[2,2]{1,0:T(2,128)} %ice_in.1, bf16[2,256,256]{2,1,0:T(8,128)(2,1)} %vel_in.1, f32[256,256]{1,0:T(8,128)} %visc_in.1, f32[256,256]{1,0:T(8,128)} %fric_in.1, ...), custom_call_target="tpu_custom_call" | custom-call | tf_op jit(solution)/shard_map/pallas_call | solution.py:460
  85.1 1.7 %copy.11 = f32[256,256]{1,0:T(8,128)} copy(f32[256,256]{1,0:T(8,128)} %shard_map.91) | data formatting | bytes 524288

commit v6 on v5

--- a/solution.py
+++ b/solution.py
@@ -54,8 +54,15 @@
             src_ref=src, dst_ref=dst, send_sem=send, recv_sem=recv, device_id=device, device_id_type=MESH
         )
 
+    def component_of(c):
+        return lax.rem(c, 2)
+
+    def offset_of(c):
+        return lax.rem((c // 2) * (chunks // 2 - 1), chunks // 2) * ROWS
+
     def rows(c):
-        return pl.ds(pl.multiple_of(c * ROWS, ROWS), ROWS)
+        start = component_of(c) * (chunks // 2 * ROWS) + offset_of(c)
+        return pl.ds(pl.multiple_of(start, ROWS), ROWS)
 
     def own_load(c):
         return pltpu.make_async_copy(obs_ref.at[:, rows(c), :], ag.at[0, c], own_sem.at[c])
@@ -143,19 +150,28 @@
             packed = block if packed is None else jnp.where(lane == n, block, packed)
         return packed.T
 
-    def send_edges(e, u, v, visc=None):
+    def send_rows(e, u, v, visc=None):
         for r, array in enumerate((u, v)):
             edge[e, 0, r : r + 1, :] = array[0:1, :]
             edge[e, 1, r : r + 1, :] = array[cells - 1 :, :]
+        if visc is not None:
+            edge[e, 1, 2:3, :] = visc[cells - 1 :, :]
+        for place in (0, 1, 4, 5):
+            edge_send(e, place).start()
+
+    def send_columns(e, u, v, visc=None):
         columns = [(False, u), (False, v), (True, u), (True, v)]
         if visc is not None:
-            edge[e, 1, 2:3, :] = visc[cells - 1 :, :]
             columns.append((True, visc))
         turned = columns_of(*columns)
         edge[e, 2, 0:2, :] = turned[0:2]
         edge[e, 3, 0:3, :] = turned[2:5]
-        for place in range(6):
+        for place in (2, 3):
             edge_send(e, place).start()
+
+    def send_edges(*field):
+        send_rows(*field)
+        send_columns(*field)
 
     def outside(e, u_first, v_first):
         for place in range(6):
@@ -273,7 +289,7 @@
         def field(r, rows_i):
             return lift[r, rows_i, :]
 
-        send_edges(2, lift.at[0], lift.at[1])
+        send_columns(2, lift.at[0], lift.at[1])
 
         def apply(rows_i, lifted, push):
             fric = fric_ref[rows_i, :]
@@ -380,8 +396,7 @@
             ring_send(side, 4, c).wait_recv()
         obs_sum = part[c, 0] + (rp[2, c] + rm[2, c])
         tile = cells // 2
-        component = c // (chunks // 2)
-        offset = lax.rem(c, chunks // 2) * ROWS
+        component, offset = component_of(c), offset_of(c)
         for s in range(SLOTS):
             at = (
                 component,
@@ -434,6 +449,7 @@
 
         pl.when(k == 1 + 4 * GAP)(finish_w)
         at_chunk(k - 1 - 4 * GAP, finish)
+        pl.when(k == 4 + 4 * GAP)(lambda: send_rows(2, lift.at[0], lift.at[1]))
         for stage in (4, 3, 2):
             at_chunk(k - 1 - (stage - 1) * GAP, functools.partial(ring_step, stage))
             pl.when(k == 2 * stage - 3)(functools.partial(ring_step_w, stage))

time: 87.3 us -> 84.7 us (0.970)
  Pallas kernels: 85.1 us -> 82.6 us
    pallas_call x1, Pallas kernels: 85.1 us -> 82.6 us  [body(): pl.pallas_call(exchange_kernel, out_shape=jax.ShapeDtypeStruct((cells, ce...]
where the time goes in v6:
time: 84.7 us; the launch traced here: 84.3 us
  Pallas kernels  82.6 us (98%)
  local copies, waits for them, and re-layouts  1.67 us (2%)
    pallas_call x1, Pallas kernels, body(): pl.pallas_call(exchange_kernel, out_shape=jax.ShapeDtypeStruct((cells, ce...  82.6 us

profile of v6, /device:TPU:1, one launch (start us, length us, event | category | flops | bytes accessed | tf_op | source)
XLA Modules:
  0.0 84.3 jit_solution(7159345106949530857)
XLA Ops:
  0.0 82.6 %shard_map.91 = f32[256,256]{1,0:T(8,128)} custom-call(s32[1,16]{1,0:T(1,128)} %bitcast.3, s32[1,16]{1,0:T(1,128)} %slot_in.1, bf16[1,16]{1,0:T(2,128)(2,1)} %weight_in.1, s32[2,2]{1,0:T(2,128)} %ice_in.1, bf16[2,256,256]{2,1,0:T(8,128)(2,1)} %vel_in.1, f32[256,256]{1,0:T(8,128)} %visc_in.1, f32[256,256]{1,0:T(8,128)} %fric_in.1, ...), custom_call_target="tpu_custom_call" | custom-call | tf_op jit(solution)/shard_map/pallas_call | solution.py:476
  82.6 1.7 %copy.11 = f32[256,256]{1,0:T(8,128)} copy(f32[256,256]{1,0:T(8,128)} %shard_map.91) | data formatting | bytes 524288

commit v7 on v6

--- a/solution.py
+++ b/solution.py
@@ -419,16 +419,15 @@
             ring_send_w(side, 4).wait_recv()
         part_w[0] += rw[3] + rw[7]
 
+    def drain(c):
+        for side in range(2):
+            own_send(side, c).wait_send()
+            far_send(side, c).wait_send()
+            for stage in range(1, 5):
+                ring_send(side, stage, c).wait_send()
+
     def wait_sends():
-        def drain(c, carry):
-            for side in range(2):
-                own_send(side, c).wait_send()
-                far_send(side, c).wait_send()
-                for stage in range(1, 5):
-                    ring_send(side, stage, c).wait_send()
-            return carry
-
-        lax.fori_loop(0, chunks, drain, 0)
+        drain(chunks - 1)
         for peer in range(3):
             meta_send(peer).wait_send()
         for side in range(2):
@@ -449,6 +448,7 @@
 
         pl.when(k == 1 + 4 * GAP)(finish_w)
         at_chunk(k - 1 - 4 * GAP, finish)
+        at_chunk(k - 2 - 4 * GAP, drain)
         pl.when(k == 4 + 4 * GAP)(lambda: send_rows(2, lift.at[0], lift.at[1]))
         for stage in (4, 3, 2):
             at_chunk(k - 1 - (stage - 1) * GAP, functools.partial(ring_step, stage))

time: 84.7 us -> 84.7 us (level)
  no operation moved by 1% of the time
where the time goes in v7:
time: 84.7 us; the launch traced here: 84.3 us
  Pallas kernels  82.7 us (98%)
  local copies, waits for them, and re-layouts  1.67 us (2%)
    pallas_call x1, Pallas kernels, body(): pl.pallas_call(exchange_kernel, out_shape=jax.ShapeDtypeStruct((cells, ce...  82.7 us

profile of v7, /device:TPU:1, one launch (start us, length us, event | category | flops | bytes accessed | tf_op | source)
XLA Modules:
  0.0 84.3 jit_solution(15450746599551591140)
XLA Ops:
  0.0 82.7 %shard_map.91 = f32[256,256]{1,0:T(8,128)} custom-call(s32[1,16]{1,0:T(1,128)} %bitcast.3, s32[1,16]{1,0:T(1,128)} %slot_in.1, bf16[1,16]{1,0:T(2,128)(2,1)} %weight_in.1, s32[2,2]{1,0:T(2,128)} %ice_in.1, bf16[2,256,256]{2,1,0:T(8,128)(2,1)} %vel_in.1, f32[256,256]{1,0:T(8,128)} %visc_in.1, f32[256,256]{1,0:T(8,128)} %fric_in.1, ...), custom_call_target="tpu_custom_call" | custom-call | tf_op jit(solution)/shard_map/pallas_call | solution.py:476
  82.7 1.7 %copy.11 = f32[256,256]{1,0:T(8,128)} copy(f32[256,256]{1,0:T(8,128)} %shard_map.91) | data formatting | bytes 524288

commit v8 on v7

--- a/solution.py
+++ b/solution.py
@@ -454,8 +454,8 @@
             at_chunk(k - 1 - (stage - 1) * GAP, functools.partial(ring_step, stage))
             pl.when(k == 2 * stage - 3)(functools.partial(ring_step_w, stage))
         at_chunk(k - 1, combine)
-        pl.when(k == 0)(first_sweep)
-        pl.when(k == 2)(second_sweep)
+        pl.when(k == 2)(first_sweep)
+        pl.when(k == 6)(second_sweep)
         return carry
 
     lax.fori_loop(0, chunks + 1 + 4 * GAP, step, 0)

time: 84.7 us -> 84.1 us (level)
  no operation moved by 1% of the time
where the time goes in v8:
time: 84.1 us; the launch traced here: 83.8 us
  Pallas kernels  82.1 us (98%)
  local copies, waits for them, and re-layouts  1.67 us (2%)
    pallas_call x1, Pallas kernels, body(): pl.pallas_call(exchange_kernel, out_shape=jax.ShapeDtypeStruct((cells, ce...  82.1 us

profile of v8, /device:TPU:1, one launch (start us, length us, event | category | flops | bytes accessed | tf_op | source)
XLA Modules:
  0.0 83.8 jit_solution(6951099145861840850)
XLA Ops:
  0.0 82.1 %shard_map.91 = f32[256,256]{1,0:T(8,128)} custom-call(s32[1,16]{1,0:T(1,128)} %bitcast.3, s32[1,16]{1,0:T(1,128)} %slot_in.1, bf16[1,16]{1,0:T(2,128)(2,1)} %weight_in.1, s32[2,2]{1,0:T(2,128)} %ice_in.1, bf16[2,256,256]{2,1,0:T(8,128)(2,1)} %vel_in.1, f32[256,256]{1,0:T(8,128)} %visc_in.1, f32[256,256]{1,0:T(8,128)} %fric_in.1, ...), custom_call_target="tpu_custom_call" | custom-call | tf_op jit(solution)/shard_map/pallas_call | solution.py:476
  82.1 1.7 %copy.11 = f32[256,256]{1,0:T(8,128)} copy(f32[256,256]{1,0:T(8,128)} %shard_map.91) | data formatting | bytes 524288
